TPU v7x, 128 devices: a whole 4x4x4 slice. The times are simulated.
128 devices in a mesh: slab: 32 (over y, z, core), tile: 4 (over x).
Axes of the slice: x: 4, y: 4, z: 4, core: 2. Of those that a mesh axis runs over, the one named last changes fastest.
Arguments:
- volume: bfloat16 [16, 256, 128, 128], P(None, 'slab', 'tile'), may hold values from -8 to 8
- first_kernel: bfloat16 [16, 4, 3, 3, 3], replicated, may hold values from -0.625 to 0.625
- second_kernel: bfloat16 [16, 4, 3, 3, 3], replicated, may hold values from -0.625 to 0.625
- density_weight: float32 [16], replicated, may hold values from -4 to 4
- upsample_kernel: bfloat16 [3, 3, 16, 16], replicated, may hold values from -4 to 4
- color_weight: bfloat16 [16, 3], replicated, may hold values from -3 to 3
Outputs:
- rendered: float32 [3, 256, 256], P(None, 'tile')
All inputs are finite; a program needn't handle non-finite values.
Results may differ from a plain program's by a relative error of at most 0.0052.
Values may be sent and summed in bfloat16 or wider, within the bound.
A program may use at most 128 MiB of HBM per device.

v0:
```python
import jax
import jax.numpy as jnp
from jax import lax
from jax.sharding import PartitionSpec as P

GROUPS = 4


row_taps = (((1, 0),), ((0, 1), (2, 0)))


def extended_2(cells, sides, width):
    for axis, dim in sides:
        count = lax.axis_size(axis)
        ends = count - 1
        head = lax.slice_in_dim(cells, 0, width, axis=dim)
        tail = lax.slice_in_dim(cells, cells.shape[dim] - width, cells.shape[dim], axis=dim)
        cells = jnp.concatenate(
            [
                lax.ppermute(tail, axis, [(i, (i + 1) % count) for i in range(ends)]),
                cells,
                lax.ppermute(head, axis, [((i + 1) % count, i) for i in range(ends)]),
            ],
            axis=dim,
        )
    return cells


def entering(value, axis, join, neutral):
    count, mine = (lax.axis_size(axis), lax.axis_index(axis))
    pieces = lax.all_gather(value, axis)
    subtotal = jnp.full_like(value, 0) + jnp.asarray(neutral, value.dtype)

    def lap(position, subtotal):
        longer = join(subtotal, pieces[position])
        return jnp.where(position < mine, longer, subtotal)

    return lax.fori_loop(0, count - 1, lap, subtotal)


def shifted(value, axis, steps):
    count = lax.axis_size(axis)
    initial, last = (max(0, -steps), min(count, count - steps))
    return lax.ppermute(value, axis, [(source, source + steps) for source in range(initial, last)])


def convolve(field, kernel, dilation):
    group_width = kernel.shape[1]
    outputs = []
    for group in range(GROUPS):
        piece = field[group * group_width : (group + 1) * group_width]
        weights = kernel[group * group_width : (group + 1) * group_width]
        outputs.append(
            lax.conv_general_dilated(
                piece[None],
                weights,
                (1, 1, 1),
                "VALID",
                rhs_dilation=(dilation, dilation, dilation),
                dimension_numbers=("NCDHW", "OIDHW", "NCDHW"),
                preferred_element_type=jnp.float32,
            )[0]
        )
    return jnp.concatenate(outputs, axis=0)


def decode(shaded, next_row, upsample_kernel, color_weight):
    height = shaded.shape[1]
    breadth = shaded.shape[2]
    extended = jnp.pad(jnp.concatenate([shaded, next_row], axis=1), ((0, 0), (0, 0), (0, 1)))
    outputs = upsample_kernel.shape[3]
    row_pieces = []
    for row_side in range(2):
        col_pieces = []
        for col_side in range(2):
            summed = jnp.zeros((outputs, height, breadth), jnp.float32)
            for row_tap, row_off in row_taps[row_side]:
                for col_tap, col_off in row_taps[col_side]:
                    window = extended[:, row_off : row_off + height, col_off : col_off + breadth]
                    summed = summed + jnp.einsum(
                        "cij,co->oij",
                        window,
                        upsample_kernel[row_tap, col_tap],
                        preferred_element_type=jnp.float32,
                    )
            col_pieces.append(summed)
        row_pieces.append(jnp.stack(col_pieces, axis=-1))
    stacked = jnp.stack(row_pieces, axis=2)
    spread = stacked.reshape(outputs, 2 * height, 2 * breadth)
    hidden = jax.nn.gelu(spread).astype(jnp.bfloat16)
    return jnp.einsum("cij,co->oij", hidden, color_weight, preferred_element_type=jnp.float32)


def add_terms(earlier, later):
    return earlier + later


def body(volume, first_kernel, second_kernel, density_weight, upsample_kernel, color_weight):
    depth_cells = volume.shape[1]
    slab_count = lax.axis_size("slab")
    slab_index = lax.axis_index("slab")
    padded = extended_2(volume, (("slab", 1), ("tile", 2)), 1)
    padded = jnp.pad(padded, ((0, 0), (0, 0), (0, 0), (1, 1)))
    hidden_field = jax.nn.gelu(convolve(padded, first_kernel, 1)).astype(jnp.bfloat16)
    widened = extended_2(hidden_field, (("slab", 1), ("tile", 2)), 2)
    widened = jnp.pad(widened, ((0, 0), (0, 0), (0, 0), (2, 2)))
    features = convolve(widened, second_kernel, 2)
    logits = jnp.einsum("c,czhw->zhw", density_weight, features, precision=lax.Precision.HIGHEST)
    depth_index = (slab_index * depth_cells + jnp.arange(depth_cells)).astype(jnp.float32)
    spacing = 1.0 + 2.0 * depth_index / (depth_cells * slab_count - 1)
    optical = jax.nn.softplus(logits) * spacing[:, None, None]
    slab_sum = jnp.sum(optical, axis=0)
    ray_total = lax.psum(slab_sum, "slab")
    earlier = entering(slab_sum, "slab", add_terms, jnp.zeros_like(slab_sum))
    local_before = jnp.cumsum(optical, axis=0) - optical
    weights = jnp.exp(-local_before / ray_total) * (1.0 - jnp.exp(-optical / ray_total))
    local_picture = jnp.einsum("zhw,czhw->chw", weights, features, precision=lax.Precision.HIGHEST)
    partial_picture = local_picture * jnp.exp(-earlier / ray_total)[None]
    shaded = lax.psum(partial_picture, "slab").astype(jnp.bfloat16)
    next_row = shifted(shaded[:, :1, :], "tile", -1)
    return decode(shaded, next_row, upsample_kernel, color_weight)


def solution(mesh):
    placed = (P(None, "slab", "tile", None), P(), P(), P(), P(), P())
    return jax.shard_map(
        body, mesh=mesh, in_specs=placed, out_specs=P(None, "tile", None), check_vma=False
    )
```

profile of v0, /device:TPU:1, one launch (start us, length us, event | category | flops | bytes accessed | tf_op | source)
XLA Modules:
  0.0 814.1 jit_solution(3985588351069389037)
XLA Ops:
  1.0 4.9 collective-permute-start
  17.0 3.7 collective-permute-done.3
  27.9 7.4 copy.213
  36.9 27.1 %broadcast_select_fusion.7 = f32[8,32,8,17,4]{2,4,3,1,0:T(4,128)} fusion(pred[8,17]{0,1:T(8,128)(4,1)S(1)} %copy-done.16, bf16[4,10,34,1,7,2]{4,0,5,2,1,3:T(4,128)(2,1)S(1)} %slice.175, bf16[4,10,34,1,8,17]{4,0,5,2,1,3:T(4,128)(2,1)} %copy.213, bf16[16,4,3,3,3]{0,1,4,3,2:T(4,128)(2,1)S(1)} %copy-done.11), kind=kOutput, calls=%fused_computation.52 | convolution fusion | flops 31460608 | bytes 968648 | tf_op jit(solution)/shard_map/conv_general_dilated | solution.py:54
  64.0 8.3 %copy.215 = f32[8,32,8,17,4]{1,0,4,3,2:T(8,128)S(1)} copy(f32[8,32,8,17,4]{2,4,3,1,0:T(4,128)} %broadcast_select_fusion.7) | data formatting | bytes 1114112 | tf_op jit(solution)/shard_map/conv_general_dilated | solution.py:54
  81.6 7.4 copy.218
  90.6 27.9 %broadcast_select_fusion.6 = f32[8,32,8,17,4]{2,4,3,1,0:T(4,128)} fusion(pred[8,17]{0,1:T(8,128)(4,1)S(1)} %copy-done.16, bf16[4,10,34,1,7,2]{4,0,5,2,1,3:T(4,128)(2,1)S(1)} %slice.178, bf16[4,10,34,1,8,17]{4,0,5,2,1,3:T(4,128)(2,1)} %copy.218, bf16[16,4,3,3,3]{0,1,4,3,2:T(4,128)(2,1)S(1)} %copy-done.12), kind=kOutput, calls=%fused_computation.51 | convolution fusion | flops 31460608 | bytes 968648 | tf_op jit(solution)/shard_map/conv_general_dilated | solution.py:54
  118.5 8.3 %copy.220 = f32[8,32,8,17,4]{1,0,4,3,2:T(8,128)S(1)} copy(f32[8,32,8,17,4]{2,4,3,1,0:T(4,128)} %broadcast_select_fusion.6) | data formatting | bytes 1114112 | tf_op jit(solution)/shard_map/conv_general_dilated | solution.py:54
  134.8 7.4 copy.223
  143.7 27.8 %broadcast_select_fusion.5 = f32[8,32,8,17,4]{2,4,3,1,0:T(4,128)} fusion(pred[8,17]{0,1:T(8,128)(4,1)S(1)} %copy-done.16, bf16[4,10,34,1,7,2]{4,0,5,2,1,3:T(4,128)(2,1)S(1)} %slice.181, bf16[4,10,34,1,8,17]{4,0,5,2,1,3:T(4,128)(2,1)} %copy.223, bf16[16,4,3,3,3]{0,1,4,3,2:T(4,128)(2,1)S(1)} %copy-done.13), kind=kOutput, calls=%fused_computation.50 | convolution fusion | flops 31460608 | bytes 968648 | tf_op jit(solution)/shard_map/conv_general_dilated | solution.py:54
  171.5 8.3 %copy.225 = f32[8,32,8,17,4]{1,0,4,3,2:T(8,128)S(1)} copy(f32[8,32,8,17,4]{2,4,3,1,0:T(4,128)} %broadcast_select_fusion.5) | data formatting | bytes 1114112 | tf_op jit(solution)/shard_map/conv_general_dilated | solution.py:54
  187.7 7.4 copy.228
  196.7 28.2 %broadcast_select_fusion.4 = f32[8,32,8,17,4]{2,4,3,1,0:T(4,128)} fusion(pred[8,17]{0,1:T(8,128)(4,1)S(1)} %copy-done.16, bf16[4,10,34,1,7,2]{4,0,5,2,1,3:T(4,128)(2,1)S(1)} %slice.184, bf16[4,10,34,1,8,17]{4,0,5,2,1,3:T(4,128)(2,1)} %copy.228, bf16[16,4,3,3,3]{0,1,4,3,2:T(4,128)(2,1)S(1)} %copy-done.14), kind=kOutput, calls=%fused_computation.49 | convolution fusion | flops 31460608 | bytes 968648 | tf_op jit(solution)/shard_map/conv_general_dilated | solution.py:54
  224.8 8.3 %copy.230 = f32[8,32,8,17,4]{1,0,4,3,2:T(8,128)S(1)} copy(f32[8,32,8,17,4]{2,4,3,1,0:T(4,128)} %broadcast_select_fusion.4) | data formatting | bytes 1114112 | tf_op jit(solution)/shard_map/conv_general_dilated | solution.py:54
  245.6 4.4 collective-permute-done.5
  267.2 8.9 %copy.240 = bf16[4,12,36,1,8,17]{4,0,5,2,1,3:T(4,128)(2,1)} copy(bf16[4,12,36,1,8,17]{2,0,5,4,1,3:T(4,128)(2,1)S(1)} %bitcast.216) | data formatting | bytes 940032 | tf_op jit(solution)/shard_map/conv_general_dilated | solution.py:54
  278.6 33.4 %broadcast_select_fusion.3 = f32[8,32,8,17,4]{2,4,3,1,0:T(4,128)} fusion(pred[8,17]{0,1:T(8,128)(4,1)S(1)} %copy-done.16, bf16[4,12,36,1,7,4]{4,0,5,2,1,3:T(4,128)(2,1)S(1)} %slice.191, bf16[4,12,36,1,8,17]{4,0,5,2,1,3:T(4,128)(2,1)} %copy.240, bf16[16,4,3,3,3]{0,1,4,3,2:T(4,128)(2,1)S(1)} %copy-done.15), kind=kOutput, calls=%fused_computation.48 | convolution fusion | flops 31962112 | bytes 1127432 | tf_op jit(solution)/shard_map/conv_general_dilated | solution.py:54
  312.0 8.3 %copy.242 = f32[8,32,8,17,4]{1,0,4,3,2:T(8,128)S(1)} copy(f32[8,32,8,17,4]{2,4,3,1,0:T(4,128)} %broadcast_select_fusion.3) | data formatting | bytes 1114112 | tf_op jit(solution)/shard_map/conv_general_dilated | solution.py:54
  329.3 8.9 %copy.245 = bf16[4,12,36,1,8,17]{4,0,5,2,1,3:T(4,128)(2,1)} copy(bf16[4,12,36,1,8,17]{2,0,5,4,1,3:T(4,128)(2,1)S(1)} %bitcast.217) | data formatting | bytes 940032 | tf_op jit(solution)/shard_map/conv_general_dilated | solution.py:54
  340.7 34.0 %broadcast_select_fusion.2 = f32[8,32,8,17,4]{2,4,3,1,0:T(4,128)} fusion(pred[8,17]{0,1:T(8,128)(4,1)S(1)} %copy-done.16, bf16[4,12,36,1,7,4]{4,0,5,2,1,3:T(4,128)(2,1)S(1)} %slice.194, bf16[4,12,36,1,8,17]{4,0,5,2,1,3:T(4,128)(2,1)} %copy.245, bf16[16,4,3,3,3]{0,1,4,3,2:T(4,128)(2,1)S(1)} %copy-done.15), kind=kOutput, calls=%fused_computation.47 | convolution fusion | flops 31962112 | bytes 1127432 | tf_op jit(solution)/shard_map/conv_general_dilated | solution.py:54
  374.6 8.3 %copy.247 = f32[8,32,8,17,4]{1,0,4,3,2:T(8,128)S(1)} copy(f32[8,32,8,17,4]{2,4,3,1,0:T(4,128)} %broadcast_select_fusion.2) | data formatting | bytes 1114112 | tf_op jit(solution)/shard_map/conv_general_dilated | solution.py:54
  391.9 8.9 %copy.250 = bf16[4,12,36,1,8,17]{4,0,5,2,1,3:T(4,128)(2,1)} copy(bf16[4,12,36,1,8,17]{2,0,5,4,1,3:T(4,128)(2,1)S(1)} %bitcast.218) | data formatting | bytes 940032 | tf_op jit(solution)/shard_map/conv_general_dilated | solution.py:54
  403.3 33.3 %broadcast_select_fusion.1 = f32[8,32,8,17,4]{2,4,3,1,0:T(4,128)} fusion(pred[8,17]{0,1:T(8,128)(4,1)S(1)} %copy-done.16, bf16[4,12,36,1,7,4]{4,0,5,2,1,3:T(4,128)(2,1)S(1)} %slice.197, bf16[4,12,36,1,8,17]{4,0,5,2,1,3:T(4,128)(2,1)} %copy.250, bf16[16,4,3,3,3]{0,1,4,3,2:T(4,128)(2,1)S(1)} %copy-done.15), kind=kOutput, calls=%fused_computation.46 | convolution fusion | flops 31962112 | bytes 1127432 | tf_op jit(solution)/shard_map/conv_general_dilated | solution.py:54
  436.6 8.3 %copy.252 = f32[8,32,8,17,4]{1,0,4,3,2:T(8,128)S(1)} copy(f32[8,32,8,17,4]{2,4,3,1,0:T(4,128)} %broadcast_select_fusion.1) | data formatting | bytes 1114112 | tf_op jit(solution)/shard_map/conv_general_dilated | solution.py:54
  453.9 8.9 %copy.255 = bf16[4,12,36,1,8,17]{4,0,5,2,1,3:T(4,128)(2,1)} copy(bf16[4,12,36,1,8,17]{2,0,5,4,1,3:T(4,128)(2,1)S(1)} %bitcast.215) | data formatting | bytes 940032 | tf_op jit(solution)/shard_map/conv_general_dilated | solution.py:54
  465.3 34.2 %broadcast_select_fusion = f32[8,32,8,17,4]{2,4,3,1,0:T(4,128)} fusion(pred[8,17]{0,1:T(8,128)(4,1)S(1)} %copy-done.16, bf16[4,12,36,1,7,4]{4,0,5,2,1,3:T(4,128)(2,1)S(1)} %slice.200, bf16[4,12,36,1,8,17]{4,0,5,2,1,3:T(4,128)(2,1)} %copy.255, bf16[16,4,3,3,3]{0,1,4,3,2:T(4,128)(2,1)S(1)} %copy-done.15), kind=kOutput, calls=%fused_computation.45 | convolution fusion | flops 31962112 | bytes 1127432 | tf_op jit(solution)/shard_map/conv_general_dilated | solution.py:54
  499.5 8.3 %copy.257 = f32[8,32,8,17,4]{1,0,4,3,2:T(8,128)S(1)} copy(f32[8,32,8,17,4]{2,4,3,1,0:T(4,128)} %broadcast_select_fusion) | data formatting | bytes 1114112 | tf_op jit(solution)/shard_map/conv_general_dilated | solution.py:54
  515.9 28.7 %all-gather = f32[1024,128]{1,0:T(8,128)S(1)} all-gather(f32[32,128]{1,0:T(8,128)S(1)} %fusion.107), channel_id=2, replica_groups=mesh['slab'=32,'tile'=4] {'slab'}, dimensions={0}, use_global_device_ids=true | all-gather | bytes 540672 | tf_op jit(solution)/shard_map/all_gather | solution.py:31
  544.6 120.9 %psum.14 = f32[32,128]{1,0:T(8,128)S(1)} all-reduce(f32[32,128]{1,0:T(8,128)S(1)} %fusion.107), channel_id=1, replica_groups=mesh['slab'=32,'tile'=4] {'slab'}, use_global_device_ids=true, to_apply=%region_2.3 | all-reduce | flops 4096 | bytes 32768 | tf_op jit(solution)/shard_map/psum | solution.py:113
  667.4 125.2 %all-reduce.4 = bf16[16,32,128]{2,0,1:T(8,128)(2,1)S(1)} all-reduce(f32[16,32,128]{2,0,1:T(8,128)S(1)} %fusion.103), channel_id=1, replica_groups=mesh['slab'=32,'tile'=4] {'slab'}, use_global_device_ids=true, to_apply=%region_5.6 | all-reduce | flops 65536 | bytes 393216 | tf_op jit(solution)/shard_map/psum | solution.py:119
  799.3 7.9 copy.271
  807.2 5.3 copy.276
  (160 shorter events, 135.3 us)
Async XLA Ops:
  0.0 812.8 %copy-start = (bf16[16,3]{0,1:T(4,128)(2,1)S(1)}, bf16[16,3]{0,1:T(4,128)(2,1)}, u32[]{:S(2)}) copy-start(bf16[16,3]{0,1:T(4,128)(2,1)} %param.13) | copy-start | bytes 292
  1.0 6.9 collective-permute-start
  5.9 6.3 collective-permute-start.1
  12.4 4.6 collective-permute-start.2
  15.5 5.2 collective-permute-start.3
  27.2 9.7 %copy-start.16 = (pred[8,17]{0,1:T(8,128)(4,1)S(1)}, pred[8,17]{0,1:T(8,128)(4,1)}, u32[]{:S(2)}) copy-start(pred[8,17]{0,1:T(8,128)(4,1)} %constant.100) | copy-start | bytes 412
  27.9 9.0 %copy-start.11 = (bf16[16,4,3,3,3]{0,1,4,3,2:T(4,128)(2,1)S(1)}, bf16[16,4,3,3,3]{0,1,4,3,2:T(4,128)(2,1)}, u32[]{:S(2)}) copy-start(bf16[16,4,3,3,3]{0,1,4,3,2:T(4,128)(2,1)} %param.9) | copy-start | bytes 10372
  81.6 9.0 %copy-start.12 = (bf16[16,4,3,3,3]{0,1,4,3,2:T(4,128)(2,1)S(1)}, bf16[16,4,3,3,3]{0,1,4,3,2:T(4,128)(2,1)}, u32[]{:S(2)}) copy-start(bf16[16,4,3,3,3]{0,1,4,3,2:T(4,128)(2,1)} %param.9) | copy-start | bytes 10372
  134.1 9.7 %copy-start.13 = (bf16[16,4,3,3,3]{0,1,4,3,2:T(4,128)(2,1)S(1)}, bf16[16,4,3,3,3]{0,1,4,3,2:T(4,128)(2,1)}, u32[]{:S(2)}) copy-start(bf16[16,4,3,3,3]{0,1,4,3,2:T(4,128)(2,1)} %param.9) | copy-start | bytes 10372
  179.8 5.0 copy-start.4
  187.0 9.7 %copy-start.14 = (bf16[16,4,3,3,3]{0,1,4,3,2:T(4,128)(2,1)S(1)}, bf16[16,4,3,3,3]{0,1,4,3,2:T(4,128)(2,1)}, u32[]{:S(2)}) copy-start(bf16[16,4,3,3,3]{0,1,4,3,2:T(4,128)(2,1)} %param.9) | copy-start | bytes 10372
  233.1 4.2 copy-start.5
  233.1 4.2 copy-start.6
  239.1 6.5 collective-permute-start.4
  242.3 7.7 collective-permute-start.5
  251.3 5.0 collective-permute-start.6
  254.4 5.4 collective-permute-start.7
  267.2 11.4 %copy-start.15 = (bf16[16,4,3,3,3]{0,1,4,3,2:T(4,128)(2,1)S(1)}, bf16[16,4,3,3,3]{0,1,4,3,2:T(4,128)(2,1)}, u32[]{:S(2)}) copy-start(bf16[16,4,3,3,3]{0,1,4,3,2:T(4,128)(2,1)} %param.10) | copy-start | bytes 10372
  507.8 4.3 copy-start.1
  507.8 4.3 copy-start.2
  507.8 5.6 copy-start.10
  507.8 8.0 copy-start.9
  509.3 156.2 %copy-start.7 = (f32[32,128]{1,0:T(8,128)S(1)}, f32[32,128]{1,0:T(8,128)}, u32[]{:S(2)}) copy-start(f32[32,128]{1,0:T(8,128)} %custom-call) | copy-start | bytes 49156
  509.3 157.6 %copy-start.3 = (f32[4,8,32,128]{3,2,1,0:T(8,128)S(1)}, f32[4,8,32,128]{3,2,1,0:T(8,128)}, u32[]{:S(2)}) copy-start(f32[4,8,32,128]{3,2,1,0:T(8,128)} %copy.260) | copy-start | bytes 1572868
  512.1 280.5 %copy-start.8 = (bf16[3,3,16,16]{3,2,1,0:T(8,128)(2,1)S(1)}, bf16[3,3,16,16]{3,2,1,0:T(8,128)(2,1)}, u32[]{:S(2)}) copy-start(bf16[3,3,16,16]{3,2,1,0:T(8,128)(2,1)} %param.12) | copy-start | bytes 13828
  793.0 4.6 collective-permute-start.8
where the time goes:
time: 830 us; the launch traced here: 814 us
  blocking collectives  275 us (33%)
  matrix products  251 us (30%)
  local copies, waits for them, and re-layouts  235 us (28%)
  starting transfers between devices  22.1 us (3%)
  waiting for transfers between devices  19.2 us (2%)
  other arithmetic  10.4 us (1%)
    conv_general_dilated x8, matrix products, convolve(): lax.conv_general_dilated(piece[None], weights, (1, 1, 1), 'VALID', rhs_di...  246 us
    conv_general_dilated x24, local copies, waits for them, and re-layouts, convolve(): lax.conv_general_dilated(piece[None], weights, (1, 1, 1), 'VALID', rhs_di...  148 us
    psum x1, blocking collectives, body(): shaded = lax.psum(partial_picture, 'slab').astype(jnp.bfloat16)  125 us
    psum x1, blocking collectives, body(): ray_total = lax.psum(slab_sum, 'slab')  121 us
    squeeze x16, local copies, waits for them, and re-layouts, convolve(): lax.conv_general_dilated(piece[None], weights, (1, 1, 1), 'VALID', rhs_di...  38.2 us
    all_gather x1, blocking collectives, entering(): pieces = lax.all_gather(value, axis)  28.7 us
    unnamed x44, local copies, waits for them, and re-layouts  23.1 us
  transfers between devices with their start and end apart: 9, of which 7 were waited for; matrix products, arithmetic and copies ran while one was open for 0% of the time, Pallas kernels for 0%

commit v1 on v0

v1 whole, which is shorter than its diff:
```python
import jax
import jax.numpy as jnp
from jax import lax
from jax.experimental import pallas as pl
from jax.experimental.pallas import tpu as pltpu
from jax.sharding import PartitionSpec as P

MESH = pl.DeviceIdType.MESH
F32 = jnp.float32
BF16 = jnp.bfloat16


def gelu(x):
    inner = x * (0.7978845608028654 + (0.7978845608028654 * 0.044715) * (x * x))
    half = 0.5 * x
    return half * jnp.tanh(inner) + half


def softplus(x):
    t = jnp.exp(-jnp.abs(x))
    tail = jnp.where(t < 1e-3, t * (1.0 - 0.5 * t), jnp.log(1.0 + t))
    return jnp.maximum(x, 0.0) + tail


def kernel(ns, nt, base_ref, dw_ref, up_ref, col_ref, vol_ref, out_ref,
           v_ref, f_ref, e_ref, rx_ref, hs_ref, xb_ref, hb_ref, w1_ref, w2f_ref, w2_ref,
           fe_ref, op_ref, tsf_ref, ts_ref, tr_ref, ti_ref, ea_ref, ps_ref, sb_ref, rb_ref, rb2_ref,
           acc_ref, im_ref, gsf_ref, gs_ref, gb_ref, gf_ref,
           vol_sem, hs_sem, hr_sem, send_sem, t_sem, r_sem, r2_sem, r2s_sem, g_sem):
    slab = lax.axis_index("slab")
    tile = lax.axis_index("tile")
    up, down = lax.rem(slab + 1, ns), lax.rem(slab + ns - 1, ns)
    east, west = lax.rem(tile + 1, nt), lax.rem(tile + nt - 1, nt)

    barrier = pltpu.get_barrier_semaphore()

    def greet(s, t):
        pl.semaphore_signal(barrier, inc=1, device_id=(s, t), device_id_type=MESH)

    for t in (east, west):
        for s in (slab, up, down):
            greet(s, t)

    @pl.loop(1, ns)
    def _(d):
        greet(lax.rem(slab + d, ns), tile)

    @pl.when(slab == ns - 1)
    def _():
        @pl.loop(0, ns)
        def _(s):
            greet(s, east)

    own = pltpu.make_async_copy(vol_ref, v_ref.at[:, 4:12], vol_sem)
    own.start()

    row = lax.broadcasted_iota(jnp.int32, (32, 128), 0)
    lane = lax.broadcasted_iota(jnp.int32, (32, 128), 1)
    z_out = lax.rem(row, 16)
    z_in = lax.rem(lane, 16)
    first = slab * 8 - 4
    keep = (z_out >= 2) & (z_out < 14) & (z_out + first >= 0) & (z_out + first < 8 * ns)
    keep = keep & (z_in + first >= 0) & (z_in + first < 8 * ns)

    @pl.loop(0, 12)
    def _(gc):
        g, c = gc // 3, lax.rem(gc, 3)
        for o in range(4):
            for half in range(2):
                line = base_ref[pl.ds((gc * 4 + o) * 2 + half, 1), :]
                band = pltpu.roll(jnp.broadcast_to(line, (32, 128)), 0, 1, stride=1, stride_axis=0)
                w1_ref[g, pl.ds(pl.multiple_of(c * 128 + o * 32, 32), 32), half * 128:half * 128 + 128] = (
                    jnp.where(keep, band, 0.0).astype(BF16))
                line = base_ref[pl.ds(96 + (gc * 4 + o) * 2 + half, 1), :]
                for hh in range(2):
                    band = pltpu.roll(jnp.broadcast_to(line, (8, 128)), hh * 16 + 2, 1, stride=1, stride_axis=0)
                    w2f_ref[g, half, pl.ds(c * 64 + o * 2 + hh, 8, stride=8), :] = band

    for half in range(2):
        w2_ref[:, :, half * 128:half * 128 + 128] = w2f_ref[:, half].astype(BF16)

    irow = lax.broadcasted_iota(jnp.int32, (256, 256), 0)
    icol = lax.broadcasted_iota(jnp.int32, (256, 256), 1)
    im_ref[...] = jnp.where(icol == 2 * lax.rem(irow, 128) + irow // 128, 1.0, 0.0).astype(BF16)

    pl.semaphore_wait(barrier, (ns - 1) + 6 + 1)
    halos = []

    def send(src, dst, n, s, t):
        copy = pltpu.make_async_remote_copy(src_ref=src, dst_ref=dst, send_sem=hs_sem.at[n], recv_sem=hr_sem.at[n],
                                            device_id=(s, t), device_id_type=MESH)
        copy.start()
        halos.append(copy)

    send(vol_ref.at[:, 5:8], v_ref.at[:, 1:4], 0, up, tile)
    send(vol_ref.at[:, 0:3], v_ref.at[:, 12:15], 1, down, tile)

    own.wait()

    @pl.loop(0, 16)
    def _(c):
        f_ref[c, 0:32, :] = jnp.zeros((32, 128), F32)
        f_ref[c, 480:512, :] = jnp.zeros((32, 128), F32)
        f_ref[c, 128:384, :] = v_ref[c, 4:12].reshape(256, 128).astype(F32)
        for side in range(2):
            for k in range(3):
                h = 29 * side + k
                for zh in range(2):
                    e_ref[side, zh, c * 3 + k] = f_ref[c, pl.ds((4 + 4 * zh) * 32 + h, 4, stride=32), :].astype(BF16)

    send(e_ref.at[1], rx_ref.at[0, 1:3], 2, slab, east)
    send(e_ref.at[0], rx_ref.at[1, 1:3], 3, slab, west)
    send(e_ref.at[1, 1], rx_ref.at[0, 0], 4, up, east)
    send(e_ref.at[1, 0], rx_ref.at[0, 3], 5, down, east)
    send(e_ref.at[0, 1], rx_ref.at[1, 0], 6, up, west)
    send(e_ref.at[0, 0], rx_ref.at[1, 3], 7, down, west)

    halos[0].wait()
    halos[1].wait()

    @pl.loop(0, 16)
    def _(c):
        f_ref[c, 32:128, :] = v_ref[c, 1:4].reshape(96, 128).astype(F32)
        f_ref[c, 384:480, :] = v_ref[c, 12:15].reshape(96, 128).astype(F32)
        for h in range(32):
            xb_ref[c, h + 3] = f_ref[c, pl.ds(h, 16, stride=32), :].astype(BF16)

    for copy in halos[2:]:
        copy.wait()
    inside = (tile > 0, tile < nt - 1)

    @pl.loop(0, 16)
    def _(c):
        for side in range(2):
            for k in range(3):
                for blk in range(4):
                    hs_ref[side, c * 3 + k, 4 * blk:4 * blk + 4, :] = rx_ref[side, blk, c * 3 + k].astype(F32)
                xb_ref[c, 35 * side + k] = jnp.where(inside[side], hs_ref[side, c * 3 + k], 0.0).astype(BF16)

    wlane = lax.broadcasted_iota(jnp.int32, (128, 128), 1)

    @pl.loop(0, 9)
    def _(j):
        for g in range(4):
            data = jnp.concatenate(
                [xb_ref[4 * g:4 * g + 4, pl.ds(4 * j + 2 * n, 4)].reshape(256, 128) for n in range(2)], axis=1)
            y = jnp.dot(w1_ref[g], data, preferred_element_type=F32)
            for n in range(2):
                part = y[:, n * 128:n * 128 + 128]
                total = part[128:256]
                total = total + jnp.where(wlane == 0, 0.0, pltpu.roll(part[0:128], 1, 1))
                total = total + jnp.where(wlane == 127, 0.0, pltpu.roll(part[256:384], 127, 1))
                hb_ref[4 * g:4 * g + 4, :, 2 * j + n] = gelu(total).astype(BF16).reshape(4, 2, 16, 128)

    @pl.when(tile == 0)
    def _():
        hb_ref[:, :, 0] = jnp.zeros((16, 2, 16, 128), BF16)

    @pl.when(tile == nt - 1)
    def _():
        hb_ref[:, :, 17] = jnp.zeros((16, 2, 16, 128), BF16)

    wlane2 = lax.broadcasted_iota(jnp.int32, (64, 128), 1)

    @pl.loop(0, 8)
    def _(k):
        for g in range(4):
            data = jnp.concatenate(
                [hb_ref[4 * g:4 * g + 4, p, pl.ds(2 * k, 4)].reshape(256, 128) for p in range(2)], axis=1)
            y = jnp.dot(w2_ref[g], data, preferred_element_type=F32)
            for p in range(2):
                part = y[:, p * 128:p * 128 + 128]
                total = part[64:128]
                total = total + jnp.where(wlane2 < 2, 0.0, pltpu.roll(part[0:64], 2, 1))
                total = total + jnp.where(wlane2 >= 126, 0.0, pltpu.roll(part[128:192], 126, 1))
                fe_ref[2 * k + p, g] = total.reshape(8, 8, 128)

    sub = lax.broadcasted_iota(jnp.int32, (8, 128), 0)
    chan = sub // 2
    dwv = []
    for g in range(4):
        v = jnp.where(chan == 0, dw_ref[4 * g], 0.0)
        for o in range(1, 4):
            v = jnp.where(chan == o, dw_ref[4 * g + o], v)
        dwv.append(v)

    @pl.loop(0, 4)
    def _(j):
        packed = jnp.zeros((8, 128), F32)
        for q in range(4):
            wi = 4 * j + q
            subtotal = jnp.zeros((8, 128), F32)
            for z in range(8):
                x = dwv[0] * fe_ref[wi, 0, z]
                for g in range(1, 4):
                    x = x + dwv[g] * fe_ref[wi, g, z]
                x = x + pltpu.roll(x, 4, 0)
                x = x + pltpu.roll(x, 2, 0)
                depth = (slab * 8 + z).astype(F32)
                optical = softplus(x) * (1.0 + 2.0 * depth / (8 * ns - 1))
                op_ref[wi, z] = optical
                subtotal = subtotal + optical
            packed = jnp.where(chan == q, subtotal, packed)
        tsf_ref[pl.ds(pl.multiple_of(8 * j, 8), 8), :] = packed

    ts_ref[...] = tsf_ref[...].astype(BF16)
    tr_ref[slab] = tsf_ref[...].astype(BF16)

    def ring(src, dst, recv, d):
        peer = lax.rem(slab + d, ns)
        return pltpu.make_async_remote_copy(src_ref=src(peer), dst_ref=dst, send_sem=send_sem.at[peer],
                                            recv_sem=recv.at[slab], device_id=(peer, tile), device_id_type=MESH)

    def arrive(src, dst, recv, d):
        peer = lax.rem(slab + d, ns)
        copy = pltpu.make_async_remote_copy(src_ref=src(peer), dst_ref=dst.at[peer], send_sem=send_sem.at[peer],
                                            recv_sem=recv.at[peer], device_id=(peer, tile), device_id_type=MESH)
        copy.wait_recv()
        copy.wait_send()

    @pl.loop(1, ns)
    def _(d):
        ring(lambda peer: ts_ref, tr_ref.at[slab], t_sem, d).start()

    @pl.loop(1, ns)
    def _(d):
        arrive(lambda peer: ts_ref, tr_ref, t_sem, d)

    def gather(s, carry):
        total, earlier = carry
        x = tr_ref[s].astype(F32)
        return total + x, earlier + jnp.where(s < slab, x, 0.0)

    zero = jnp.zeros((32, 128), F32)
    total, earlier = lax.fori_loop(0, ns, gather, (zero, zero))
    ti_ref[...] = 1.0 / total
    ea_ref[...] = earlier

    @pl.loop(0, 4)
    def _(j):
        rows = pl.ds(pl.multiple_of(8 * j, 8), 8)
        inverse4, before4 = ti_ref[rows, :], ea_ref[rows, :]
        for q in range(4):
            wi = 4 * j + q

            def spread(v):
                v = jnp.where(chan == q, v, 0.0)
                v = v + pltpu.roll(v, 4, 0)
                return v + pltpu.roll(v, 2, 0)

            inverse, before = spread(inverse4), spread(before4)
            through = jnp.exp(-before * inverse)
            sums = [jnp.zeros((8, 128), F32)] * 4
            for z in range(8):
                before = before + op_ref[wi, z]
                after = jnp.exp(-before * inverse)
                weight = through - after
                through = after
                for g in range(4):
                    sums[g] = sums[g] + weight * fe_ref[wi, g, z]
            for g in range(4):
                ps_ref[wi, 8 * g:8 * g + 8, :] = sums[g]

    @pl.loop(0, 8)
    def _(k):
        for p in range(2):
            for hh in range(2):
                sb_ref[4 * k + 2 * hh + p] = ps_ref[2 * k + p, pl.ds(hh, 16, stride=2), :].astype(BF16)
    sb_ref[32] = jnp.zeros((16, 128), BF16)

    @pl.loop(1, ns)
    def _(d):
        ring(lambda peer: sb_ref.at[pl.ds(peer, 2)], rb_ref.at[slab], r_sem, d).start()

    below = pltpu.make_async_remote_copy(src_ref=sb_ref.at[0], dst_ref=rb2_ref.at[slab], send_sem=r2s_sem,
                                         recv_sem=r2_sem.at[slab], device_id=(ns - 1, west), device_id_type=MESH)
    below.start()
    rb_ref[slab] = sb_ref[pl.ds(slab, 2)]

    @pl.loop(1, ns)
    def _(d):
        arrive(lambda peer: sb_ref.at[pl.ds(peer, 2)], rb_ref, r_sem, d)

    below.wait_send()

    def collect(s, carry):
        return carry + rb_ref[s].astype(F32)

    acc_ref[...] = lax.fori_loop(0, ns, collect, jnp.zeros((2, 16, 128), F32))

    @pl.when(slab == ns - 1)
    def _():
        @pl.loop(0, ns)
        def _(s):
            pltpu.make_async_remote_copy(src_ref=sb_ref.at[0], dst_ref=rb2_ref.at[s], send_sem=r2s_sem,
                                         recv_sem=r2_sem.at[s], device_id=(ns - 1, west),
                                         device_id_type=MESH).wait_recv()

        def collect2(s, carry):
            return carry + rb2_ref[s].astype(F32)

        below_row = lax.fori_loop(0, ns, collect2, jnp.zeros((16, 128), F32))
        acc_ref[1] = jnp.where(tile < nt - 1, below_row, 0.0)

    lane16 = lax.broadcasted_iota(jnp.int32, (16, 128), 1)
    shaded = []
    for r in range(2):
        s = acc_ref[r].astype(BF16)
        s32 = s.astype(F32)
        right = jnp.where(lane16 == 127, 0.0, pltpu.roll(s32, 127, 1)).astype(BF16)
        shaded.append((s, right))

    def contract(a, b):
        return lax.dot_general(a, b, (((0,), (0,)), ((), ())), preferred_element_type=F32)

    taps = (((1, 0),), ((0, 1), (2, 0)))
    gsf_ref[...] = jnp.zeros((8, 256), F32)
    for a in range(2):
        pair = []
        for b in range(2):
            y = jnp.zeros((16, 128), F32)
            for r, p in taps[a]:
                for s, q in taps[b]:
                    y = y + contract(up_ref[r, s], shaded[p][q])
            hidden = gelu(y).astype(BF16)
            pair.append(contract(col_ref[...], hidden).astype(BF16))
        line = jnp.dot(jnp.concatenate(pair, axis=1), im_ref[...], preferred_element_type=F32)
        gsf_ref[4 * a:4 * a + 3, :] = line
    gs_ref[...] = gsf_ref[...].astype(BF16)
    gb_ref[slab] = gsf_ref[...].astype(BF16)

    @pl.loop(1, ns)
    def _(d):
        ring(lambda peer: gs_ref, gb_ref.at[slab], g_sem, d).start()

    @pl.loop(1, ns)
    def _(d):
        arrive(lambda peer: gs_ref, gb_ref, g_sem, d)

    for half in range(2):
        @pl.loop(0, ns)
        def _(s):
            gf_ref[half, pl.ds(pl.multiple_of(8 * s, 8), 8), :] = gb_ref[s, :, half * 128:half * 128 + 128].astype(F32)

        for color in range(3):
            for a in range(2):
                out_ref[color, half, pl.ds(a, 32, stride=2), :] = gf_ref[half, pl.ds(4 * a + color, 32, stride=8), :]


def bases(first_kernel, second_kernel):
    lines = []
    for kern, gap in ((first_kernel, 0), (second_kernel, 1)):
        k = kern.astype(F32).reshape(4, 4, 4, 3, 3, 3)
        k = k.transpose(0, 5, 1, 2, 4, 3)
        wide = 3 + 2 * gap
        k = lax.pad(k, jnp.float32(0), [(0, 0, 0)] * 4 + [(0, 1, 0), (0, 16 - wide, gap)])
        lines.append(jnp.roll(k.reshape(96, 128), gap - 1, axis=1))
    return jnp.concatenate(lines, axis=0)


def solution(mesh):
    ns, nt = mesh.shape["slab"], mesh.shape["tile"]

    def body(volume, first_kernel, second_kernel, density_weight, upsample_kernel, color_weight):
        vmem = pl.BlockSpec(memory_space=pltpu.VMEM)
        dma = pltpu.SemaphoreType.DMA
        out = pl.pallas_call(
            lambda *refs: kernel(ns, nt, *refs),
            out_shape=jax.ShapeDtypeStruct((3, 2, 64, 128), F32),
            in_specs=[vmem, pl.BlockSpec(memory_space=pltpu.SMEM), vmem, vmem, pl.BlockSpec(memory_space=pl.ANY)],
            out_specs=vmem,
            scratch_shapes=[
                pltpu.VMEM((16, 16, 32, 128), BF16),
                pltpu.VMEM((16, 512, 128), F32),
                pltpu.VMEM((2, 2, 48, 4, 128), BF16),
                pltpu.VMEM((2, 4, 48, 4, 128), BF16),
                pltpu.VMEM((2, 48, 16, 128), F32),
                pltpu.VMEM((16, 38, 16, 128), BF16),
                pltpu.VMEM((16, 2, 18, 16, 128), BF16),
                pltpu.VMEM((4, 384, 256), BF16),
                pltpu.VMEM((4, 2, 192, 128), F32),
                pltpu.VMEM((4, 192, 256), BF16),
                pltpu.VMEM((16, 4, 8, 8, 128), F32),
                pltpu.VMEM((16, 8, 8, 128), F32),
                pltpu.VMEM((32, 128), F32),
                pltpu.VMEM((32, 128), BF16),
                pltpu.VMEM((ns, 32, 128), BF16),
                pltpu.VMEM((32, 128), F32),
                pltpu.VMEM((32, 128), F32),
                pltpu.VMEM((16, 32, 128), F32),
                pltpu.VMEM((ns + 1, 16, 128), BF16),
                pltpu.VMEM((ns, 2, 16, 128), BF16),
                pltpu.VMEM((ns, 16, 128), BF16),
                pltpu.VMEM((2, 16, 128), F32),
                pltpu.VMEM((256, 256), BF16),
                pltpu.VMEM((8, 256), F32),
                pltpu.VMEM((8, 256), BF16),
                pltpu.VMEM((ns, 8, 256), BF16),
                pltpu.VMEM((2, 8 * ns, 128), F32),
                dma, dma((8,)), dma((8,)), dma((ns,)), dma((ns,)), dma((ns,)), dma((ns,)), dma, dma((ns,)),
            ],
            compiler_params=pltpu.CompilerParams(
                collective_id=0, has_side_effects=True, vmem_limit_bytes=60 * 2**20),
        )(bases(first_kernel, second_kernel), density_weight, upsample_kernel, color_weight, volume)
        return out.transpose(0, 2, 1, 3).reshape(3, 64, 256)

    placed = (P(None, "slab", "tile", None), P(), P(), P(), P(), P())
    return jax.shard_map(
        body, mesh=mesh, in_specs=placed, out_specs=P(None, "tile", None), check_vma=False
    )
```

time: 830 us -> 77.2 us (0.09); the launches traced: 814 us -> 77 us
  blocking collectives: 275 us -> 0 us
  matrix products: 251 us -> 0 us
  local copies, waits for them, and re-layouts: 235 us -> 23.5 us
  Pallas kernels: 0 us -> 52.5 us
  starting transfers between devices: 22.1 us -> 0 us
  waiting for transfers between devices: 19.2 us -> 0 us
  other arithmetic: 10.4 us -> 0.85 us
    psum x2 -> x0, blocking collectives: 246 us -> none  [the longest x1 125 us: body(): shaded = lax.psum(partial_picture, 'slab').astype(jnp.bfloat16)]
    conv_general_dilated x8 -> x0, matrix products: 246 us -> none  [convolve(): lax.conv_general_dilated(piece[None], weights, (1, 1, 1), 'VALID', rhs_di...]
    conv_general_dilated x24 -> x0, local copies, waits for them, and re-layouts: 148 us -> none  [convolve(): lax.conv_general_dilated(piece[None], weights, (1, 1, 1), 'VALID', rhs_di...]
    pallas_call x0 -> x1, Pallas kernels: none -> 52.5 us  [body(): pl.pallas_call(lambda *refs: kernel(ns, nt, *refs), out_shape=jax.ShapeDt...]
    squeeze x16 -> x0, local copies, waits for them, and re-layouts: 38.2 us -> none  [convolve(): lax.conv_general_dilated(piece[None], weights, (1, 1, 1), 'VALID', rhs_di...]
    all_gather x1 -> x0, blocking collectives: 28.7 us -> none  [entering(): pieces = lax.all_gather(value, axis)]
    ppermute x9 -> x0, starting transfers between devices: 22.1 us -> none  [the longest x4 14.4 us: extended_2(): lax.ppermute(tail, axis, [(i, (i + 1) % count) for i in range(ends)])]
    unnamed x44 -> x5, local copies, waits for them, and re-layouts: 23.1 us -> 1.35 us
  transfers between devices with their start and end apart: 9 -> 0, of which waited for: 7 -> 0; matrix products, arithmetic and copies ran while one was open for 0% -> 0% of each run, Pallas kernels for 0% -> 0%
where the time goes in v1:
time: 77.2 us; the launch traced here: 77 us
  Pallas kernels  52.5 us (68%)
  local copies, waits for them, and re-layouts  23.5 us (30%)
  other arithmetic  0.85 us (1%)
    pallas_call x1, Pallas kernels, body(): pl.pallas_call(lambda *refs: kernel(ns, nt, *refs), out_shape=jax.ShapeDt...  52.5 us
    pad x1, local copies, waits for them, and re-layouts, bases(): lax.pad(k, jnp.float32(0), [(0, 0, 0)] * 4 + [(0, 1, 0), (0, 16 - wide, g...  16.3 us
    reshape x4, local copies, waits for them, and re-layouts, bases(): k = kern.astype(F32).reshape(4, 4, 4, 3, 3, 3)  3.69 us
    reshape x1, local copies, waits for them, and re-layouts, body(): return out.transpose(0, 2, 1, 3).reshape(3, 64, 256)  1.62 us

profile of v1, /device:TPU:1, one launch (start us, length us, event | category | flops | bytes accessed | tf_op | source)
XLA Modules:
  0.0 77.0 jit_solution(7669391417660176068)
XLA Ops:
  0.0 0.9 %reshape.23 = bf16[4,4,4,3,3,3]{1,0,2,5,4,3:T(4,128)(2,1)S(1)} reshape(bf16[16,4,3,3,3]{0,1,4,3,2:T(4,128)(2,1)} %param.7) | data formatting | bytes 6912 | tf_op jit(solution)/shard_map/reshape | solution.py:353
  0.9 1.4 %copy.10 = bf16[4,4,4,3,3,3]{3,4,2,1,5,0:T(4,128)(2,1)S(1)} copy(bf16[4,4,4,3,3,3]{1,0,2,5,4,3:T(4,128)(2,1)S(1)} %reshape.23) | data formatting | bytes 6912 | tf_op jit(solution)/shard_map/reshape | solution.py:353
  2.2 0.1 pad_convert_fusion
  2.4 0.3 reshape.31
  2.6 0.0 copy-start
  2.6 0.1 slice.10
  2.7 0.7 copy-done
  3.4 0.1 reshape.26
  3.5 1.4 %copy.11 = bf16[4,4,4,3,3,3]{3,4,2,1,5,0:T(4,128)(2,1)S(1)} copy(bf16[4,4,4,3,3,3]{1,0,2,5,4,3:T(4,128)(2,1)S(1)} %reshape.26) | data formatting | bytes 6912 | tf_op jit(solution)/shard_map/reshape | solution.py:353
  4.8 16.3 %pad.9 = bf16[4,3,4,4,4,16]{5,4,3,2,1,0:T(4,128)(2,1)S(1)} pad(bf16[4,3,4,4,3,3]{5,4,3,2,1,0:T(4,128)(2,1)S(1)} %bitcast.13, bf16[]{:T(256)} %constant.2.clone.1), padding=0_0_0x0_0_0x0_0_0x0_0_0x0_1_0x0_11_1 | pad | bytes 28034 | tf_op jit(solution)/shard_map/pad | solution.py:356
  21.2 0.2 reshape.33
  21.4 0.0 copy-start.1
  21.4 0.7 pad_maximum_fusion.refs_0_
  22.1 0.0 copy-done.1
  22.1 0.7 copy.12.refs_3_
  22.8 52.5 %shard_map.64 = f32[3,2,64,128]{3,2,1,0:T(8,128)} custom-call(f32[192,128]{1,0:T(8,128)} %pad_maximum_fusion.refs_0_, f32[16]{0:T(128)} %refs_1_.1, bf16[3,3,16,16]{3,2,1,0:T(8,128)(2,1)} %refs_2_.1, bf16[16,3]{1,0:T(8,128)(2,1)} %copy.12.refs_3_, bf16[16,8,32,128]{3,2,1,0:T(8,128)(2,1)} %refs_4_.1), custom_call_target="tpu_custom_call" | custom-call | tf_op jit(solution)/shard_map/pallas_call | solution.py:367
  75.3 1.6 %copy_bitcast_fusion = f32[3,64,256]{2,1,0:T(8,128)} fusion(f32[3,2,64,128]{3,2,1,0:T(8,128)} %shard_map.64), kind=kLoop, calls=%fused_computation | loop fusion | bytes 393216 | tf_op jit(solution)/shard_map/reshape | solution.py:405
Async XLA Ops:
  2.6 0.7 copy-start
  21.4 0.7 copy-start.1

commit v2 on v1

--- a/solution.py
+++ b/solution.py
@@ -16,17 +16,26 @@
     return half * jnp.tanh(inner) + half
 
 
+def gelu_of_half(y):
+    inner = y * (2 * 0.7978845608028654 + (8 * 0.7978845608028654 * 0.044715) * (y * y))
+    return y * jnp.tanh(inner) + y
+
+
+def contract(a, b):
+    return lax.dot_general(a, b, (((0,), (0,)), ((), ())), preferred_element_type=F32)
+
+
 def softplus(x):
     t = jnp.exp(-jnp.abs(x))
     tail = jnp.where(t < 1e-3, t * (1.0 - 0.5 * t), jnp.log(1.0 + t))
     return jnp.maximum(x, 0.0) + tail
 
 
-def kernel(ns, nt, base_ref, dw_ref, up_ref, col_ref, vol_ref, out_ref,
-           v_ref, f_ref, e_ref, rx_ref, hs_ref, xb_ref, hb_ref, w1_ref, w2f_ref, w2_ref,
+def kernel(ns, nt, k1_any, k2_any, dw_any, up_any, col_any, vol_ref, out_ref,
+           k1_ref, k2_ref, dw_ref, up_ref, col_ref, v_ref, f_ref, e_ref, rx_ref, hs_ref, xb_ref, hb_ref, w1_ref, w2f_ref, w2_ref,
            fe_ref, op_ref, tsf_ref, ts_ref, tr_ref, ti_ref, ea_ref, ps_ref, sb_ref, rb_ref, rb2_ref,
-           acc_ref, im_ref, gsf_ref, gs_ref, gb_ref, gf_ref,
-           vol_sem, hs_sem, hr_sem, send_sem, t_sem, r_sem, r2_sem, r2s_sem, g_sem):
+           ks_ref, base_ref, acc_ref, im_ref, gsf_ref, gs_ref, gb_ref, gf_ref, of_ref,
+           vol_sem, in_sem, hs_sem, hr_sem, send_sem, t_sem, r_sem, r2_sem, r2s_sem, g_sem):
     slab = lax.axis_index("slab")
     tile = lax.axis_index("tile")
     up, down = lax.rem(slab + 1, ns), lax.rem(slab + ns - 1, ns)
@@ -53,6 +62,51 @@
 
     own = pltpu.make_async_copy(vol_ref, v_ref.at[:, 4:12], vol_sem)
     own.start()
+    params = [pltpu.make_async_copy(src, dst, in_sem.at[n]) for n, (src, dst) in enumerate(
+        ((k1_any, k1_ref), (k2_any, k2_ref), (dw_any, dw_ref), (up_any, up_ref), (col_any, col_ref)))]
+    for copy in params:
+        copy.start()
+
+    own.wait()
+
+    @pl.loop(0, 16)
+    def _(c):
+        f_ref[c, 0:32, :] = jnp.zeros((32, 128), F32)
+        f_ref[c, 540:572, :] = jnp.zeros((32, 128), F32)
+        f_ref[c, 144:176, :] = v_ref[c, 4].astype(F32)
+        f_ref[c, 180:212, :] = v_ref[c, 5].astype(F32)
+        f_ref[c, 216:248, :] = v_ref[c, 6].astype(F32)
+        f_ref[c, 252:284, :] = v_ref[c, 7].astype(F32)
+        f_ref[c, 288:320, :] = v_ref[c, 8].astype(F32)
+        f_ref[c, 324:356, :] = v_ref[c, 9].astype(F32)
+        f_ref[c, 360:392, :] = v_ref[c, 10].astype(F32)
+        f_ref[c, 396:428, :] = v_ref[c, 11].astype(F32)
+        for side in range(2):
+            for k in range(3):
+                h = 29 * side + k
+                for zh in range(2):
+                    e_ref[side, zh, c * 3 + k] = f_ref[c, pl.ds((4 + 4 * zh) * 36 + h, 4, stride=36), :].astype(BF16)
+
+    pl.semaphore_wait(barrier, (ns - 1) + 6 + 1)
+    halos = []
+
+    def send(src, dst, n, s, t):
+        copy = pltpu.make_async_remote_copy(src_ref=src, dst_ref=dst, send_sem=hs_sem.at[n], recv_sem=hr_sem.at[n],
+                                            device_id=(s, t), device_id_type=MESH)
+        copy.start()
+        halos.append(copy)
+
+    for part in range(2):
+        rows = slice(16 * part, 16 * part + 16)
+        send(vol_ref.at[:, 5:8, rows], v_ref.at[:, 1:4, rows], 2 * part, up, tile)
+        send(vol_ref.at[:, 0:3, rows], v_ref.at[:, 12:15, rows], 2 * part + 1, down, tile)
+
+    send(e_ref.at[1], rx_ref.at[0, 1:3], 4, slab, east)
+    send(e_ref.at[0], rx_ref.at[1, 1:3], 5, slab, west)
+    send(e_ref.at[1, 1], rx_ref.at[0, 0], 6, up, east)
+    send(e_ref.at[1, 0], rx_ref.at[0, 3], 7, down, east)
+    send(e_ref.at[0, 1], rx_ref.at[1, 0], 8, up, west)
+    send(e_ref.at[0, 0], rx_ref.at[1, 3], 9, down, west)
 
     row = lax.broadcasted_iota(jnp.int32, (32, 128), 0)
     lane = lax.broadcasted_iota(jnp.int32, (32, 128), 1)
@@ -62,19 +116,35 @@
     keep = (z_out >= 2) & (z_out < 14) & (z_out + first >= 0) & (z_out + first < 8 * ns)
     keep = keep & (z_in + first >= 0) & (z_in + first < 8 * ns)
 
+    for copy in params:
+        copy.wait()
+    ks_ref[...] = jnp.zeros((2, 3, 40, 16), F32)
+    prow = lax.broadcasted_iota(jnp.int32, (40, 128), 0)
+    plane = lax.broadcasted_iota(jnp.int32, (40, 128), 1)
+    pi, pa, pb = lax.rem(prow, 4), prow // 12, lax.rem(prow // 4, 3)
+    for conv, k_ref in enumerate((k1_ref, k2_ref)):
+        for c in range(3):
+            for ab in range(9):
+                ks_ref[conv, c, 4 * ab:4 * ab + 4, :] = k_ref[ab * 3 + c].astype(F32)
+        spot = lax.rem(lax.rem(pi, 2) * 64 + pb * 16 + pa * (1 + conv) + (127 + conv), 128)
+        for half in range(2):
+            place = jnp.where((spot == plane) & (pi // 2 == half) & (prow < 36), 0.5 if conv == 0 else 1.0, 0.0).astype(BF16)
+            for c in range(3):
+                base_ref[conv, half, 16 * c:16 * c + 16, :] = contract(ks_ref[conv, c].astype(BF16), place)
+
     @pl.loop(0, 12)
     def _(gc):
         g, c = gc // 3, lax.rem(gc, 3)
         for o in range(4):
             for half in range(2):
-                line = base_ref[pl.ds((gc * 4 + o) * 2 + half, 1), :]
+                line = base_ref[0, half, pl.ds(c * 16 + g * 4 + o, 1), :]
                 band = pltpu.roll(jnp.broadcast_to(line, (32, 128)), 0, 1, stride=1, stride_axis=0)
-                w1_ref[g, pl.ds(pl.multiple_of(c * 128 + o * 32, 32), 32), half * 128:half * 128 + 128] = (
+                w1_ref[g, pl.ds(pl.multiple_of(o * 96 + c * 32, 32), 32), half * 128:half * 128 + 128] = (
                     jnp.where(keep, band, 0.0).astype(BF16))
-                line = base_ref[pl.ds(96 + (gc * 4 + o) * 2 + half, 1), :]
+                line = base_ref[1, half, pl.ds(c * 16 + g * 4 + o, 1), :]
                 for hh in range(2):
                     band = pltpu.roll(jnp.broadcast_to(line, (8, 128)), hh * 16 + 2, 1, stride=1, stride_axis=0)
-                    w2f_ref[g, half, pl.ds(c * 64 + o * 2 + hh, 8, stride=8), :] = band
+                    w2f_ref[g, half, pl.ds(c * 8 + o * 2 + hh, 8, stride=24), :] = band
 
     for half in range(2):
         w2_ref[:, :, half * 128:half * 128 + 128] = w2f_ref[:, half].astype(BF16)
@@ -83,74 +153,55 @@
     icol = lax.broadcasted_iota(jnp.int32, (256, 256), 1)
     im_ref[...] = jnp.where(icol == 2 * lax.rem(irow, 128) + irow // 128, 1.0, 0.0).astype(BF16)
 
-    pl.semaphore_wait(barrier, (ns - 1) + 6 + 1)
-    halos = []
-
-    def send(src, dst, n, s, t):
-        copy = pltpu.make_async_remote_copy(src_ref=src, dst_ref=dst, send_sem=hs_sem.at[n], recv_sem=hr_sem.at[n],
-                                            device_id=(s, t), device_id_type=MESH)
-        copy.start()
-        halos.append(copy)
-
-    send(vol_ref.at[:, 5:8], v_ref.at[:, 1:4], 0, up, tile)
-    send(vol_ref.at[:, 0:3], v_ref.at[:, 12:15], 1, down, tile)
-
-    own.wait()
-
-    @pl.loop(0, 16)
-    def _(c):
-        f_ref[c, 0:32, :] = jnp.zeros((32, 128), F32)
-        f_ref[c, 480:512, :] = jnp.zeros((32, 128), F32)
-        f_ref[c, 128:384, :] = v_ref[c, 4:12].reshape(256, 128).astype(F32)
-        for side in range(2):
-            for k in range(3):
-                h = 29 * side + k
-                for zh in range(2):
-                    e_ref[side, zh, c * 3 + k] = f_ref[c, pl.ds((4 + 4 * zh) * 32 + h, 4, stride=32), :].astype(BF16)
-
-    send(e_ref.at[1], rx_ref.at[0, 1:3], 2, slab, east)
-    send(e_ref.at[0], rx_ref.at[1, 1:3], 3, slab, west)
-    send(e_ref.at[1, 1], rx_ref.at[0, 0], 4, up, east)
-    send(e_ref.at[1, 0], rx_ref.at[0, 3], 5, down, east)
-    send(e_ref.at[0, 1], rx_ref.at[1, 0], 6, up, west)
-    send(e_ref.at[0, 0], rx_ref.at[1, 3], 7, down, west)
+    inside = (tile > 0, tile < nt - 1)
+
+    def relayout(part):
+        @pl.loop(0, 16)
+        def _(c):
+            for z in (1, 2, 3, 12, 13, 14):
+                f_ref[c, 36 * z + 16 * part:36 * z + 16 * part + 16, :] = v_ref[c, z, 16 * part:16 * part + 16].astype(F32)
+            for h in range(16 * part, 16 * part + 16):
+                xb_ref[c, h + 3] = f_ref[c, pl.ds(h, 16, stride=36), :].astype(BF16)
 
     halos[0].wait()
     halos[1].wait()
-
-    @pl.loop(0, 16)
-    def _(c):
-        f_ref[c, 32:128, :] = v_ref[c, 1:4].reshape(96, 128).astype(F32)
-        f_ref[c, 384:480, :] = v_ref[c, 12:15].reshape(96, 128).astype(F32)
-        for h in range(32):
-            xb_ref[c, h + 3] = f_ref[c, pl.ds(h, 16, stride=32), :].astype(BF16)
-
-    for copy in halos[2:]:
-        copy.wait()
-    inside = (tile > 0, tile < nt - 1)
-
-    @pl.loop(0, 16)
-    def _(c):
-        for side in range(2):
-            for k in range(3):
-                for blk in range(4):
-                    hs_ref[side, c * 3 + k, 4 * blk:4 * blk + 4, :] = rx_ref[side, blk, c * 3 + k].astype(F32)
-                xb_ref[c, 35 * side + k] = jnp.where(inside[side], hs_ref[side, c * 3 + k], 0.0).astype(BF16)
-
-    wlane = lax.broadcasted_iota(jnp.int32, (128, 128), 1)
+    relayout(0)
+
+    wlane = lax.broadcasted_iota(jnp.int32, (32, 128), 1)
 
     @pl.loop(0, 9)
-    def _(j):
+    def _(i):
+        @pl.when(i == 3)
+        def _():
+            halos[2].wait()
+            halos[3].wait()
+            relayout(1)
+
+        @pl.when(i == 7)
+        def _():
+            for copy in halos[4:]:
+                copy.wait()
+
+            @pl.loop(0, 16)
+            def _(c):
+                for side in range(2):
+                    for k in range(3):
+                        for blk in range(4):
+                            hs_ref[side, c * 3 + k, 4 * blk:4 * blk + 4, :] = rx_ref[side, blk, c * 3 + k].astype(F32)
+                        xb_ref[c, 35 * side + k] = jnp.where(inside[side], hs_ref[side, c * 3 + k], 0.0).astype(BF16)
+
+        j = lax.rem(i + 1, 8) + 7 * (i // 8)
         for g in range(4):
             data = jnp.concatenate(
                 [xb_ref[4 * g:4 * g + 4, pl.ds(4 * j + 2 * n, 4)].reshape(256, 128) for n in range(2)], axis=1)
             y = jnp.dot(w1_ref[g], data, preferred_element_type=F32)
-            for n in range(2):
-                part = y[:, n * 128:n * 128 + 128]
-                total = part[128:256]
-                total = total + jnp.where(wlane == 0, 0.0, pltpu.roll(part[0:128], 1, 1))
-                total = total + jnp.where(wlane == 127, 0.0, pltpu.roll(part[256:384], 127, 1))
-                hb_ref[4 * g:4 * g + 4, :, 2 * j + n] = gelu(total).astype(BF16).reshape(4, 2, 16, 128)
+            for o in range(4):
+                for n in range(2):
+                    part = y[96 * o:96 * o + 96, n * 128:n * 128 + 128]
+                    total = part[32:64]
+                    total = total + jnp.where(wlane == 0, 0.0, pltpu.roll(part[0:32], 1, 1))
+                    total = total + jnp.where(wlane == 127, 0.0, pltpu.roll(part[64:96], 127, 1))
+                    hb_ref[4 * g + o, :, 2 * j + n] = gelu_of_half(total).astype(BF16).reshape(2, 16, 128)
 
     @pl.when(tile == 0)
     def _():
@@ -160,7 +211,7 @@
     def _():
         hb_ref[:, :, 17] = jnp.zeros((16, 2, 16, 128), BF16)
 
-    wlane2 = lax.broadcasted_iota(jnp.int32, (64, 128), 1)
+    wlane2 = lax.broadcasted_iota(jnp.int32, (8, 128), 1)
 
     @pl.loop(0, 8)
     def _(k):
@@ -168,12 +219,13 @@
             data = jnp.concatenate(
                 [hb_ref[4 * g:4 * g + 4, p, pl.ds(2 * k, 4)].reshape(256, 128) for p in range(2)], axis=1)
             y = jnp.dot(w2_ref[g], data, preferred_element_type=F32)
-            for p in range(2):
-                part = y[:, p * 128:p * 128 + 128]
-                total = part[64:128]
-                total = total + jnp.where(wlane2 < 2, 0.0, pltpu.roll(part[0:64], 2, 1))
-                total = total + jnp.where(wlane2 >= 126, 0.0, pltpu.roll(part[128:192], 126, 1))
-                fe_ref[2 * k + p, g] = total.reshape(8, 8, 128)
+            for z in range(8):
+                for p in range(2):
+                    part = y[24 * z:24 * z + 24, p * 128:p * 128 + 128]
+                    total = part[8:16]
+                    total = total + jnp.where(wlane2 < 2, 0.0, pltpu.roll(part[0:8], 2, 1))
+                    total = total + jnp.where(wlane2 >= 126, 0.0, pltpu.roll(part[16:24], 126, 1))
+                    fe_ref[2 * k + p, g, z] = total
 
     sub = lax.broadcasted_iota(jnp.int32, (8, 128), 0)
     chan = sub // 2
@@ -310,9 +362,6 @@
         right = jnp.where(lane16 == 127, 0.0, pltpu.roll(s32, 127, 1)).astype(BF16)
         shaded.append((s, right))
 
-    def contract(a, b):
-        return lax.dot_general(a, b, (((0,), (0,)), ((), ())), preferred_element_type=F32)
-
     taps = (((1, 0),), ((0, 1), (2, 0)))
     gsf_ref[...] = jnp.zeros((8, 256), F32)
     for a in range(2):
@@ -323,7 +372,7 @@
                 for s, q in taps[b]:
                     y = y + contract(up_ref[r, s], shaded[p][q])
             hidden = gelu(y).astype(BF16)
-            pair.append(contract(col_ref[...], hidden).astype(BF16))
+            pair.append(jnp.dot(col_ref[...], hidden, preferred_element_type=F32).astype(BF16))
         line = jnp.dot(jnp.concatenate(pair, axis=1), im_ref[...], preferred_element_type=F32)
         gsf_ref[4 * a:4 * a + 3, :] = line
     gs_ref[...] = gsf_ref[...].astype(BF16)
@@ -344,18 +393,12 @@
 
         for color in range(3):
             for a in range(2):
-                out_ref[color, half, pl.ds(a, 32, stride=2), :] = gf_ref[half, pl.ds(4 * a + color, 32, stride=8), :]
-
-
-def bases(first_kernel, second_kernel):
-    lines = []
-    for kern, gap in ((first_kernel, 0), (second_kernel, 1)):
-        k = kern.astype(F32).reshape(4, 4, 4, 3, 3, 3)
-        k = k.transpose(0, 5, 1, 2, 4, 3)
-        wide = 3 + 2 * gap
-        k = lax.pad(k, jnp.float32(0), [(0, 0, 0)] * 4 + [(0, 1, 0), (0, 16 - wide, gap)])
-        lines.append(jnp.roll(k.reshape(96, 128), gap - 1, axis=1))
-    return jnp.concatenate(lines, axis=0)
+                of_ref[color, half, pl.ds(a, 32, stride=2), :] = gf_ref[half, pl.ds(4 * a + color, 32, stride=8), :]
+            out_ref[color, :, half * 128:half * 128 + 128] = of_ref[color, half]
+
+
+def by_tap(kern):
+    return kern.transpose(2, 3, 4, 1, 0).reshape(27, 4, 16)
 
 
 def solution(mesh):
@@ -366,12 +409,17 @@
         dma = pltpu.SemaphoreType.DMA
         out = pl.pallas_call(
             lambda *refs: kernel(ns, nt, *refs),
-            out_shape=jax.ShapeDtypeStruct((3, 2, 64, 128), F32),
-            in_specs=[vmem, pl.BlockSpec(memory_space=pltpu.SMEM), vmem, vmem, pl.BlockSpec(memory_space=pl.ANY)],
+            out_shape=jax.ShapeDtypeStruct((3, 64, 256), F32),
+            in_specs=[pl.BlockSpec(memory_space=pltpu.HBM)] * 6,
             out_specs=vmem,
             scratch_shapes=[
+                pltpu.VMEM((27, 4, 16), BF16),
+                pltpu.VMEM((27, 4, 16), BF16),
+                pltpu.SMEM((16,), F32),
+                pltpu.VMEM((3, 3, 16, 16), BF16),
+                pltpu.VMEM((3, 16), BF16),
                 pltpu.VMEM((16, 16, 32, 128), BF16),
-                pltpu.VMEM((16, 512, 128), F32),
+                pltpu.VMEM((16, 576, 128), F32),
                 pltpu.VMEM((2, 2, 48, 4, 128), BF16),
                 pltpu.VMEM((2, 4, 48, 4, 128), BF16),
                 pltpu.VMEM((2, 48, 16, 128), F32),
@@ -391,18 +439,22 @@
                 pltpu.VMEM((ns + 1, 16, 128), BF16),
                 pltpu.VMEM((ns, 2, 16, 128), BF16),
                 pltpu.VMEM((ns, 16, 128), BF16),
+                pltpu.VMEM((2, 3, 40, 16), F32),
+                pltpu.VMEM((2, 2, 48, 128), F32),
                 pltpu.VMEM((2, 16, 128), F32),
                 pltpu.VMEM((256, 256), BF16),
                 pltpu.VMEM((8, 256), F32),
                 pltpu.VMEM((8, 256), BF16),
                 pltpu.VMEM((ns, 8, 256), BF16),
                 pltpu.VMEM((2, 8 * ns, 128), F32),
-                dma, dma((8,)), dma((8,)), dma((ns,)), dma((ns,)), dma((ns,)), dma((ns,)), dma, dma((ns,)),
+                pltpu.VMEM((3, 2, 64, 128), F32),
+                dma, dma((5,)), dma((10,)), dma((10,)), dma((ns,)), dma((ns,)), dma((ns,)), dma((ns,)), dma, dma((ns,)),
             ],
             compiler_params=pltpu.CompilerParams(
-                collective_id=0, has_side_effects=True, vmem_limit_bytes=60 * 2**20),
-        )(bases(first_kernel, second_kernel), density_weight, upsample_kernel, color_weight, volume)
-        return out.transpose(0, 2, 1, 3).reshape(3, 64, 256)
+                collective_id=0, has_side_effects=True, vmem_limit_bytes=40 * 2**20),
+        )(*[pltpu.with_memory_space_constraint(x, pltpu.HBM) for x in (
+            by_tap(first_kernel), by_tap(second_kernel), density_weight, upsample_kernel, color_weight.T, volume)])
+        return out
 
     placed = (P(None, "slab", "tile", None), P(), P(), P(), P(), P())
     return jax.shard_map(

time: 77.2 us -> 47.5 us (0.62)
  local copies, waits for them, and re-layouts: 23.5 us -> 0.68 us
  Pallas kernels: 52.5 us -> 46.7 us
  other arithmetic: 0.85 us -> 0 us
    pad x1 -> x0, local copies, waits for them, and re-layouts: 16.3 us -> none  [bases(): lax.pad(k, jnp.float32(0), [(0, 0, 0)] * 4 + [(0, 1, 0), (0, 16 - wide, g...]
    reshape x7 -> x0, local copies, waits for them, and re-layouts: 5.79 us -> none  [the longest x4 3.69 us: bases(): k = kern.astype(F32).reshape(4, 4, 4, 3, 3, 3)]
    pallas_call x1, Pallas kernels: 52.5 us -> 46.7 us  [body(): pl.pallas_call(lambda *refs: kernel(ns, nt, *refs), out_shape=jax.ShapeDt...]
where the time goes in v2:
time: 47.5 us; the launch traced here: 47.4 us
  Pallas kernels  46.7 us (98%)
  local copies, waits for them, and re-layouts  0.68 us (1%)
    pallas_call x1, Pallas kernels, body(): pl.pallas_call(lambda *refs: kernel(ns, nt, *refs), out_shape=jax.ShapeDt...  46.7 us

profile of v2, /device:TPU:1, one launch (start us, length us, event | category | flops | bytes accessed | tf_op | source)
XLA Modules:
  0.0 47.4 jit_solution(10307521913067206972)
XLA Ops:
  0.0 46.7 %shard_map.64 = f32[3,64,256]{2,1,0:T(8,128)S(1)} custom-call(bf16[27,4,16]{2,1,0:T(4,128)(2,1)} %bitcast.7, bf16[27,4,16]{2,1,0:T(4,128)(2,1)} %bitcast.8, f32[16]{0:T(128)} %refs_2_.1, bf16[3,3,16,16]{3,2,1,0:T(8,128)(2,1)} %refs_3_.1, bf16[3,16]{1,0:T(4,128)(2,1)} %bitcast.9, bf16[16,8,32,128]{3,2,1,0:T(8,128)(2,1)} %refs_5_.1), custom_call_target="tpu_custom_call" | custom-call | tf_op jit(solution)/shard_map/pallas_call | solution.py:410
  46.7 0.7 %copy.8 = f32[3,64,256]{2,1,0:T(8,128)} copy(f32[3,64,256]{2,1,0:T(8,128)S(1)} %shard_map.64) | data formatting | bytes 393216

commit v3 on v2

v3 whole, which is shorter than its diff:
```python
import jax
import jax.numpy as jnp
from jax import lax
from jax.experimental import pallas as pl
from jax.experimental.pallas import tpu as pltpu
from jax.sharding import PartitionSpec as P

MESH = pl.DeviceIdType.MESH
F32 = jnp.float32
BF16 = jnp.bfloat16


def gelu(x):
    inner = x * (0.7978845608028654 + (0.7978845608028654 * 0.044715) * (x * x))
    half = 0.5 * x
    return half * jnp.tanh(inner) + half


def gelu_of_half(y):
    inner = y * (2 * 0.7978845608028654 + (8 * 0.7978845608028654 * 0.044715) * (y * y))
    return y * jnp.tanh(inner) + y


def contract(a, b):
    return lax.dot_general(a, b, (((0,), (0,)), ((), ())), preferred_element_type=F32)


def softplus(x):
    t = jnp.exp(-jnp.abs(x))
    tail = jnp.where(t < 1e-3, t * (1.0 - 0.5 * t), jnp.log(1.0 + t))
    return jnp.maximum(x, 0.0) + tail


def kernel(ns, nt, k1_any, k2_any, dw_any, up_any, col_any, vol_ref, out_ref,
           k1_ref, k2_ref, dw_ref, up_ref, col_ref, v_ref, f_ref, e_ref, rx_ref, hs_ref, xb_ref, hb_ref, w1f_ref, w1_ref, w2f_ref, w2_ref,
           fe_ref, op_ref, sum_ref, tsf_ref, ts_ref, tr_ref, ti_ref, ea_ref, ps_ref, sb_ref, rb_ref, rb2_ref,
           ks_ref, base_ref, acc_ref, im_ref, gsf_ref, gs_ref, gb_ref, gf_ref, of_ref,
           vol_sem, in_sem, hs_sem, hr_sem, ts_sem, t_sem, rs_sem, r_sem, r2_sem, r2s_sem, gs_sem, g_sem):
    slab = lax.axis_index("slab")
    tile = lax.axis_index("tile")
    up, down = lax.rem(slab + 1, ns), lax.rem(slab + ns - 1, ns)
    east, west = lax.rem(tile + 1, nt), lax.rem(tile + nt - 1, nt)

    barrier = pltpu.get_barrier_semaphore()

    def greet(s, t):
        pl.semaphore_signal(barrier, inc=1, device_id=(s, t), device_id_type=MESH)

    for t in (east, west):
        for s in (slab, up, down):
            greet(s, t)

    @pl.loop(1, ns)
    def _(d):
        greet(lax.rem(slab + d, ns), tile)

    @pl.when(slab == ns - 1)
    def _():
        @pl.loop(0, ns)
        def _(s):
            greet(s, east)

    own = pltpu.make_async_copy(vol_ref, v_ref.at[:, 4:12], vol_sem)
    own.start()
    params = [pltpu.make_async_copy(src, dst, in_sem.at[n]) for n, (src, dst) in enumerate(
        ((k1_any, k1_ref), (k2_any, k2_ref), (dw_any, dw_ref), (up_any, up_ref), (col_any, col_ref)))]
    for copy in params:
        copy.start()

    own.wait()

    @pl.loop(0, 16)
    def _(c):
        f_ref[c, 0:32, :] = jnp.zeros((32, 128), F32)
        f_ref[c, 540:572, :] = jnp.zeros((32, 128), F32)
        f_ref[c, 144:176, :] = v_ref[c, 4].astype(F32)
        f_ref[c, 180:212, :] = v_ref[c, 5].astype(F32)
        f_ref[c, 216:248, :] = v_ref[c, 6].astype(F32)
        f_ref[c, 252:284, :] = v_ref[c, 7].astype(F32)
        f_ref[c, 288:320, :] = v_ref[c, 8].astype(F32)
        f_ref[c, 324:356, :] = v_ref[c, 9].astype(F32)
        f_ref[c, 360:392, :] = v_ref[c, 10].astype(F32)
        f_ref[c, 396:428, :] = v_ref[c, 11].astype(F32)
        for side in range(2):
            for k in range(3):
                h = 29 * side + k
                for zh in range(2):
                    e_ref[side, zh, c * 3 + k] = f_ref[c, pl.ds((4 + 4 * zh) * 36 + h, 4, stride=36), :].astype(BF16)

    pl.semaphore_wait(barrier, (ns - 1) + 6 + 1)
    halos = []

    def send(src, dst, n, s, t):
        copy = pltpu.make_async_remote_copy(src_ref=src, dst_ref=dst, send_sem=hs_sem.at[n], recv_sem=hr_sem.at[n],
                                            device_id=(s, t), device_id_type=MESH)
        copy.start()
        halos.append(copy)

    for part in range(4):
        rows = slice(8 * part, 8 * part + 8)
        send(vol_ref.at[:, 5:8, rows], v_ref.at[:, 1:4, rows], 2 * part, up, tile)
        send(vol_ref.at[:, 0:3, rows], v_ref.at[:, 12:15, rows], 2 * part + 1, down, tile)

    send(e_ref.at[1], rx_ref.at[0, 1:3], 8, slab, east)
    send(e_ref.at[0], rx_ref.at[1, 1:3], 9, slab, west)
    send(e_ref.at[1, 1], rx_ref.at[0, 0], 10, up, east)
    send(e_ref.at[1, 0], rx_ref.at[0, 3], 11, down, east)
    send(e_ref.at[0, 1], rx_ref.at[1, 0], 12, up, west)
    send(e_ref.at[0, 0], rx_ref.at[1, 3], 13, down, west)

    row = lax.broadcasted_iota(jnp.int32, (24, 128), 0)
    lane = lax.broadcasted_iota(jnp.int32, (24, 128), 1)
    z_out = lax.rem(row, 12) + 2
    z_in = lax.rem(lane, 16)
    first = slab * 8 - 4
    keep = (z_out + first >= 0) & (z_out + first < 8 * ns)
    keep = keep & (z_in + first >= 0) & (z_in + first < 8 * ns)

    for copy in params:
        copy.wait()
    ks_ref[...] = jnp.zeros((2, 3, 40, 16), F32)
    prow = lax.broadcasted_iota(jnp.int32, (40, 128), 0)
    plane = lax.broadcasted_iota(jnp.int32, (40, 128), 1)
    pi, pa, pb = lax.rem(prow, 4), prow // 12, lax.rem(prow // 4, 3)
    for conv, k_ref in enumerate((k1_ref, k2_ref)):
        for c in range(3):
            for ab in range(9):
                ks_ref[conv, c, 4 * ab:4 * ab + 4, :] = k_ref[ab * 3 + c].astype(F32)
        spot = lax.rem(lax.rem(pi, 2) * 64 + pb * 16 + pa * (1 + conv), 128)
        for half in range(2):
            place = jnp.where((spot == plane) & (pi // 2 == half) & (prow < 36), 0.5 if conv == 0 else 1.0, 0.0).astype(BF16)
            for c in range(3):
                base_ref[conv, half, 16 * c:16 * c + 16, :] = contract(ks_ref[conv, c].astype(BF16), place)

    @pl.loop(0, 12)
    def _(gc):
        g, c = gc // 3, lax.rem(gc, 3)
        for o in range(4):
            for half in range(2):
                line = base_ref[0, half, pl.ds(c * 16 + g * 4 + o, 1), :]
                line = jnp.broadcast_to(line, (24, 128))
                band = jnp.where(row < 12, pltpu.roll(line, 1, 1, stride=1, stride_axis=0),
                                 pltpu.roll(line, 5, 1, stride=1, stride_axis=0))
                w1f_ref[g, half, pl.ds(pl.multiple_of(o * 72 + c * 24, 8), 24), :] = jnp.where(keep, band, 0.0)
                line = base_ref[1, half, pl.ds(c * 16 + g * 4 + o, 1), :]
                for hh in range(2):
                    band = pltpu.roll(jnp.broadcast_to(line, (8, 128)), hh * 16, 1, stride=1, stride_axis=0)
                    w2f_ref[g, half, pl.ds(c * 8 + o * 2 + hh, 8, stride=24), :] = band

    for half in range(2):
        w1_ref[:, :, half * 128:half * 128 + 128] = w1f_ref[:, half].astype(BF16)
        w2_ref[:, :, half * 128:half * 128 + 128] = w2f_ref[:, half].astype(BF16)

    irow = lax.broadcasted_iota(jnp.int32, (256, 256), 0)
    icol = lax.broadcasted_iota(jnp.int32, (256, 256), 1)
    im_ref[...] = jnp.where(icol == 2 * lax.rem(irow, 128) + irow // 128, 1.0, 0.0).astype(BF16)

    inside = (tile > 0, tile < nt - 1)

    sub = lax.broadcasted_iota(jnp.int32, (8, 128), 0)
    chan = sub // 2
    dwv = []
    for g in range(4):
        v = jnp.where(chan == 0, dw_ref[4 * g], 0.0)
        for o in range(1, 4):
            v = jnp.where(chan == o, dw_ref[4 * g + o], v)
        dwv.append(v)
    wlane = lax.broadcasted_iota(jnp.int32, (24, 128), 1)
    wlane2 = lax.broadcasted_iota(jnp.int32, (8, 128), 1)

    def relayout(part):
        halos[2 * part].wait()
        halos[2 * part + 1].wait()

        @pl.loop(0, 16)
        def _(c):
            for z in (1, 2, 3, 12, 13, 14):
                f_ref[c, 36 * z + 8 * part:36 * z + 8 * part + 8, :] = v_ref[c, z, 8 * part:8 * part + 8].astype(F32)
            for h in range(8 * part, 8 * part + 8):
                xb_ref[c, h + 3] = f_ref[c, pl.ds(h, 16, stride=36), :].astype(BF16)

    def first_conv(j):
        for g in range(4):
            data = jnp.concatenate(
                [xb_ref[4 * g:4 * g + 4, pl.ds(4 * j + 2 * n, 4)].reshape(256, 128) for n in range(2)], axis=1)
            y = jnp.dot(w1_ref[g], data, preferred_element_type=F32)
            for o in range(4):
                for n in range(2):
                    part = y[72 * o:72 * o + 72, n * 128:n * 128 + 128]
                    total = part[24:48]
                    total = total + jnp.where(wlane == 0, 0.0, pltpu.roll(part[0:24], 1, 1))
                    total = total + jnp.where(wlane == 127, 0.0, pltpu.roll(part[48:72], 127, 1))
                    total = gelu_of_half(total)
                    hb_ref[4 * g + o, 0, 2 * j + n] = total[0:16].astype(BF16)
                    hb_ref[4 * g + o, 1, 2 * j + n] = pltpu.roll(total, 12, 0)[0:16].astype(BF16)

    def second_conv(n):
        k = lax.rem(n + 1, 8)
        logit = [[None] * 8 for _ in range(2)]
        for g in range(4):
            data = jnp.concatenate(
                [hb_ref[4 * g:4 * g + 4, p, pl.ds(2 * k, 4)].reshape(256, 128) for p in range(2)], axis=1)
            y = jnp.dot(w2_ref[g], data, preferred_element_type=F32)
            for z in range(8):
                for p in range(2):
                    part = y[24 * z:24 * z + 24, p * 128:p * 128 + 128]
                    total = part[8:16]
                    total = total + jnp.where(wlane2 < 2, 0.0, pltpu.roll(part[0:8], 2, 1))
                    total = total + jnp.where(wlane2 >= 126, 0.0, pltpu.roll(part[16:24], 126, 1))
                    fe_ref[2 * n + p, g, z] = total
                    term = dwv[g] * total
                    logit[p][z] = term if g == 0 else logit[p][z] + term
        for p in range(2):
            subtotal = jnp.zeros((8, 128), F32)
            for z in range(8):
                x = logit[p][z]
                x = x + pltpu.roll(x, 4, 0)
                x = x + pltpu.roll(x, 2, 0)
                depth = (slab * 8 + z).astype(F32)
                optical = softplus(x) * (1.0 + 2.0 * depth / (8 * ns - 1))
                op_ref[2 * n + p, z] = optical
                subtotal = subtotal + optical
            sum_ref[2 * n + p] = subtotal

    def push(src, dst, sends, recv, peer):
        return pltpu.make_async_remote_copy(src_ref=src, dst_ref=dst, send_sem=sends, recv_sem=recv,
                                            device_id=(peer, tile), device_id_type=MESH)

    def to_all(src, dst, sends, recv):
        @pl.loop(1, ns)
        def _(d):
            push(src, dst.at[slab], sends, recv, lax.rem(slab + d, ns)).start()

    def from_all(dst, sends, recv):
        every = dst.at[pl.ds(0, ns - 1)]
        push(every, every, sends, recv, up).wait()

    def send_totals(half):
        for m in range(2):
            packed = sum_ref[8 * half + 4 * m]
            for q in range(1, 4):
                packed = jnp.where(chan == q, sum_ref[8 * half + 4 * m + q], packed)
            tsf_ref[half, 8 * m:8 * m + 8, :] = packed
        ts_ref[half] = tsf_ref[half].astype(BF16)
        tr_ref[half, slab] = tsf_ref[half].astype(BF16)
        to_all(ts_ref.at[half], tr_ref.at[half], ts_sem.at[half], t_sem.at[half])

    relayout(0)

    @pl.loop(0, 2)
    def _(i):
        @pl.when(i == 1)
        def _():
            relayout(1)

        first_conv(i + 1)

    @pl.loop(2, 9)
    def _(i):
        @pl.when(i == 3)
        def _():
            relayout(2)

        @pl.when(i == 5)
        def _():
            relayout(3)

        @pl.when(i == 6)
        def _():
            send_totals(0)

        @pl.when(i == 7)
        def _():
            for copy in halos[8:]:
                copy.wait()

            @pl.loop(0, 16)
            def _(c):
                for side in range(2):
                    for k in range(3):
                        for blk in range(4):
                            hs_ref[side, c * 3 + k, 4 * blk:4 * blk + 4, :] = rx_ref[side, blk, c * 3 + k].astype(F32)
                        xb_ref[c, 35 * side + k] = jnp.where(inside[side], hs_ref[side, c * 3 + k], 0.0).astype(BF16)

        @pl.when((i == 8) & (tile == nt - 1))
        def _():
            hb_ref[:, :, 17] = jnp.zeros((16, 2, 16, 128), BF16)

        second_conv(i - 2)
        first_conv(lax.rem(i + 1, 9))

    @pl.when(tile == 0)
    def _():
        hb_ref[:, :, 0] = jnp.zeros((16, 2, 16, 128), BF16)

    second_conv(7)
    send_totals(1)

    def shade(half):
        from_all(tr_ref.at[half], ts_sem.at[half], t_sem.at[half])

        def gather(s, carry):
            total, earlier = carry
            x = tr_ref[half, s].astype(F32)
            return total + x, earlier + jnp.where(s < slab, x, 0.0)

        zero = jnp.zeros((16, 128), F32)
        total, earlier = lax.fori_loop(0, ns, gather, (zero, zero))
        ti_ref[...] = 1.0 / total
        ea_ref[...] = earlier

        @pl.loop(0, 2)
        def _(m):
            rows = pl.ds(pl.multiple_of(8 * m, 8), 8)
            inverse4, before4 = ti_ref[rows, :], ea_ref[rows, :]
            for q in range(4):
                wi = 8 * half + 4 * m + q

                def spread(v):
                    v = jnp.where(chan == q, v, 0.0)
                    v = v + pltpu.roll(v, 4, 0)
                    return v + pltpu.roll(v, 2, 0)

                inverse, before = spread(inverse4), spread(before4)
                through = jnp.exp(-before * inverse)
                sums = [jnp.zeros((8, 128), F32)] * 4
                for z in range(8):
                    before = before + op_ref[wi, z]
                    after = jnp.exp(-before * inverse)
                    weight = through - after
                    through = after
                    for g in range(4):
                        sums[g] = sums[g] + weight * fe_ref[wi, g, z]
                for g in range(4):
                    ps_ref[wi, 8 * g:8 * g + 8, :] = sums[g]
                k = lax.rem(4 * half + 2 * m + q // 2 + 1, 8)
                for hh in range(2):
                    sb_ref[4 * k + 2 * hh + q % 2] = ps_ref[wi, pl.ds(hh, 16, stride=2), :].astype(BF16)

    def send_rows(owner):
        @pl.when(owner != slab)
        def _():
            push(sb_ref.at[pl.ds(owner, 2)], rb_ref.at[slab], rs_sem, r_sem, owner).start()

    sb_ref[32] = jnp.zeros((16, 128), BF16)
    shade(0)

    @pl.loop(0, 15)
    def _(e):
        send_rows(4 + lax.rem(slab + e, 15))

    shade(1)
    below = pltpu.make_async_remote_copy(src_ref=sb_ref.at[0], dst_ref=rb2_ref.at[slab], send_sem=r2s_sem,
                                         recv_sem=r2_sem, device_id=(ns - 1, west), device_id_type=MESH)
    below.start()

    @pl.loop(0, 17)
    def _(e):
        at = lax.rem(slab + e, 17)
        send_rows(at + 15 * ((at + 13) // 17))

    rb_ref[slab] = sb_ref[pl.ds(slab, 2)]
    from_all(rb_ref, rs_sem, r_sem)
    below.wait_send()

    def collect(s, carry):
        return carry + rb_ref[s].astype(F32)

    acc_ref[...] = lax.fori_loop(0, ns, collect, jnp.zeros((2, 16, 128), F32))

    @pl.when(slab == ns - 1)
    def _():
        pltpu.make_async_remote_copy(src_ref=rb2_ref, dst_ref=rb2_ref, send_sem=r2s_sem, recv_sem=r2_sem,
                                     device_id=(ns - 1, west), device_id_type=MESH).wait_recv()

        def collect2(s, carry):
            return carry + rb2_ref[s].astype(F32)

        below_row = lax.fori_loop(0, ns, collect2, jnp.zeros((16, 128), F32))
        acc_ref[1] = jnp.where(tile < nt - 1, below_row, 0.0)

    lane16 = lax.broadcasted_iota(jnp.int32, (16, 128), 1)
    shaded = []
    for r in range(2):
        s = acc_ref[r].astype(BF16)
        s32 = s.astype(F32)
        right = jnp.where(lane16 == 127, 0.0, pltpu.roll(s32, 127, 1)).astype(BF16)
        shaded.append((s, right))

    taps = (((1, 0),), ((0, 1), (2, 0)))
    gsf_ref[...] = jnp.zeros((8, 256), F32)
    for a in range(2):
        pair = []
        for b in range(2):
            y = jnp.zeros((16, 128), F32)
            for r, p in taps[a]:
                for s, q in taps[b]:
                    y = y + contract(up_ref[r, s], shaded[p][q])
            hidden = gelu(y).astype(BF16)
            pair.append(jnp.dot(col_ref[...], hidden, preferred_element_type=F32).astype(BF16))
        line = jnp.dot(jnp.concatenate(pair, axis=1), im_ref[...], preferred_element_type=F32)
        gsf_ref[4 * a:4 * a + 3, :] = line
    gs_ref[...] = gsf_ref[...].astype(BF16)
    gb_ref[slab] = gsf_ref[...].astype(BF16)

    to_all(gs_ref, gb_ref, gs_sem, g_sem)
    from_all(gb_ref, gs_sem, g_sem)

    for half in range(2):
        @pl.loop(0, ns)
        def _(s):
            gf_ref[half, pl.ds(pl.multiple_of(8 * s, 8), 8), :] = gb_ref[s, :, half * 128:half * 128 + 128].astype(F32)

        for color in range(3):
            for a in range(2):
                of_ref[color, half, pl.ds(a, 32, stride=2), :] = gf_ref[half, pl.ds(4 * a + color, 32, stride=8), :]
            out_ref[color, :, half * 128:half * 128 + 128] = of_ref[color, half]


def by_tap(kern):
    return kern.transpose(2, 3, 4, 1, 0).reshape(27, 4, 16)


def solution(mesh):
    ns, nt = mesh.shape["slab"], mesh.shape["tile"]

    def body(volume, first_kernel, second_kernel, density_weight, upsample_kernel, color_weight):
        vmem = pl.BlockSpec(memory_space=pltpu.VMEM)
        dma = pltpu.SemaphoreType.DMA
        out = pl.pallas_call(
            lambda *refs: kernel(ns, nt, *refs),
            out_shape=jax.ShapeDtypeStruct((3, 64, 256), F32),
            in_specs=[pl.BlockSpec(memory_space=pltpu.HBM)] * 6,
            out_specs=vmem,
            scratch_shapes=[
                pltpu.VMEM((27, 4, 16), BF16),
                pltpu.VMEM((27, 4, 16), BF16),
                pltpu.SMEM((16,), F32),
                pltpu.VMEM((3, 3, 16, 16), BF16),
                pltpu.VMEM((3, 16), BF16),
                pltpu.VMEM((16, 16, 32, 128), BF16),
                pltpu.VMEM((16, 576, 128), F32),
                pltpu.VMEM((2, 2, 48, 4, 128), BF16),
                pltpu.VMEM((2, 4, 48, 4, 128), BF16),
                pltpu.VMEM((2, 48, 16, 128), F32),
                pltpu.VMEM((16, 38, 16, 128), BF16),
                pltpu.VMEM((16, 2, 18, 16, 128), BF16),
                pltpu.VMEM((4, 2, 288, 128), F32),
                pltpu.VMEM((4, 288, 256), BF16),
                pltpu.VMEM((4, 2, 192, 128), F32),
                pltpu.VMEM((4, 192, 256), BF16),
                pltpu.VMEM((16, 4, 8, 8, 128), F32),
                pltpu.VMEM((16, 8, 8, 128), F32),
                pltpu.VMEM((16, 8, 128), F32),
                pltpu.VMEM((2, 16, 128), F32),
                pltpu.VMEM((2, 16, 128), BF16),
                pltpu.VMEM((2, ns, 16, 128), BF16),
                pltpu.VMEM((16, 128), F32),
                pltpu.VMEM((16, 128), F32),
                pltpu.VMEM((16, 32, 128), F32),
                pltpu.VMEM((ns + 1, 16, 128), BF16),
                pltpu.VMEM((ns, 2, 16, 128), BF16),
                pltpu.VMEM((ns, 16, 128), BF16),
                pltpu.VMEM((2, 3, 40, 16), F32),
                pltpu.VMEM((2, 2, 48, 128), F32),
                pltpu.VMEM((2, 16, 128), F32),
                pltpu.VMEM((256, 256), BF16),
                pltpu.VMEM((8, 256), F32),
                pltpu.VMEM((8, 256), BF16),
                pltpu.VMEM((ns, 8, 256), BF16),
                pltpu.VMEM((2, 8 * ns, 128), F32),
                pltpu.VMEM((3, 2, 64, 128), F32),
                dma, dma((5,)), dma((14,)), dma((14,)), dma((2,)), dma((2,)), dma, dma, dma, dma, dma, dma,
            ],
            compiler_params=pltpu.CompilerParams(
                collective_id=0, has_side_effects=True, vmem_limit_bytes=40 * 2**20),
        )(*[pltpu.with_memory_space_constraint(x, pltpu.HBM) for x in (
            by_tap(first_kernel), by_tap(second_kernel), density_weight, upsample_kernel, color_weight.T, volume)])
        return out

    placed = (P(None, "slab", "tile", None), P(), P(), P(), P(), P())
    return jax.shard_map(
        body, mesh=mesh, in_specs=placed, out_specs=P(None, "tile", None), check_vma=False
    )
```

time: 47.5 us -> 41.1 us (0.87)
  Pallas kernels: 46.7 us -> 40.3 us
    pallas_call x1, Pallas kernels: 46.7 us -> 40.3 us  [body(): pl.pallas_call(lambda *refs: kernel(ns, nt, *refs), out_shape=jax.ShapeDt...]
where the time goes in v3:
time: 41.1 us; the launch traced here: 41 us
  Pallas kernels  40.3 us (98%)
  local copies, waits for them, and re-layouts  0.68 us (2%)
    pallas_call x1, Pallas kernels, body(): pl.pallas_call(lambda *refs: kernel(ns, nt, *refs), out_shape=jax.ShapeDt...  40.3 us

profile of v3, /device:TPU:1, one launch (start us, length us, event | category | flops | bytes accessed | tf_op | source)
XLA Modules:
  0.0 41.0 jit_solution(729470382940847057)
XLA Ops:
  0.0 40.3 %shard_map.64 = f32[3,64,256]{2,1,0:T(8,128)S(1)} custom-call(bf16[27,4,16]{2,1,0:T(4,128)(2,1)} %bitcast.7, bf16[27,4,16]{2,1,0:T(4,128)(2,1)} %bitcast.8, f32[16]{0:T(128)} %refs_2_.1, bf16[3,3,16,16]{3,2,1,0:T(8,128)(2,1)} %refs_3_.1, bf16[3,16]{1,0:T(4,128)(2,1)} %bitcast.9, bf16[16,8,32,128]{3,2,1,0:T(8,128)(2,1)} %refs_5_.1), custom_call_target="tpu_custom_call" | custom-call | tf_op jit(solution)/shard_map/pallas_call | solution.py:430
  40.3 0.7 %copy.8 = f32[3,64,256]{2,1,0:T(8,128)} copy(f32[3,64,256]{2,1,0:T(8,128)S(1)} %shard_map.64) | data formatting | bytes 393216

commit v4 on v3

--- a/solution.py
+++ b/solution.py
@@ -33,8 +33,8 @@
 
 def kernel(ns, nt, k1_any, k2_any, dw_any, up_any, col_any, vol_ref, out_ref,
            k1_ref, k2_ref, dw_ref, up_ref, col_ref, v_ref, f_ref, e_ref, rx_ref, hs_ref, xb_ref, hb_ref, w1f_ref, w1_ref, w2f_ref, w2_ref,
-           fe_ref, op_ref, sum_ref, tsf_ref, ts_ref, tr_ref, ti_ref, ea_ref, ps_ref, sb_ref, rb_ref, rb2_ref,
-           ks_ref, base_ref, acc_ref, im_ref, gsf_ref, gs_ref, gb_ref, gf_ref, of_ref,
+           y_ref, fe_ref, op_ref, sum_ref, tsf_ref, ts_ref, tr_ref, ti_ref, ea_ref, ps_ref, sb_ref, rb_ref, rb2_ref,
+           ks_ref, base_ref, acc_ref, im_ref, gsf_ref, gs_ref, gb_ref, pm_ref,
            vol_sem, in_sem, hs_sem, hr_sem, ts_sem, t_sem, rs_sem, r_sem, r2_sem, r2s_sem, gs_sem, g_sem):
     slab = lax.axis_index("slab")
     tile = lax.axis_index("tile")
@@ -154,6 +154,10 @@
     irow = lax.broadcasted_iota(jnp.int32, (256, 256), 0)
     icol = lax.broadcasted_iota(jnp.int32, (256, 256), 1)
     im_ref[...] = jnp.where(icol == 2 * lax.rem(irow, 128) + irow // 128, 1.0, 0.0).astype(BF16)
+    prow = lax.broadcasted_iota(jnp.int32, (192, 256), 0)
+    pcol = lax.broadcasted_iota(jnp.int32, (192, 256), 1)
+    source = lax.rem(prow, 64) // 2 * 8 + lax.rem(prow, 2) * 4 + prow // 64
+    pm_ref[...] = jnp.where(pcol == source, 1.0, 0.0).astype(BF16)
 
     inside = (tile > 0, tile < nt - 1)
 
@@ -179,41 +183,69 @@
             for h in range(8 * part, 8 * part + 8):
                 xb_ref[c, h + 3] = f_ref[c, pl.ds(h, 16, stride=36), :].astype(BF16)
 
+    pending = []
+    turns = [0]
+
+    def issue(matrix, data, finish):
+        rows = matrix.shape[0]
+        place = y_ref.at[turns[0], 0:rows]
+        turns[0] = 1 - turns[0]
+        place[...] = jnp.dot(matrix, data, preferred_element_type=F32)
+        flush()
+        pending.append(lambda: finish(place))
+
+    def flush():
+        while pending:
+            pending.pop()()
+
     def first_conv(j):
         for g in range(4):
             data = jnp.concatenate(
-                [xb_ref[4 * g:4 * g + 4, pl.ds(4 * j + 2 * n, 4)].reshape(256, 128) for n in range(2)], axis=1)
-            y = jnp.dot(w1_ref[g], data, preferred_element_type=F32)
-            for o in range(4):
-                for n in range(2):
-                    part = y[72 * o:72 * o + 72, n * 128:n * 128 + 128]
-                    total = part[24:48]
-                    total = total + jnp.where(wlane == 0, 0.0, pltpu.roll(part[0:24], 1, 1))
-                    total = total + jnp.where(wlane == 127, 0.0, pltpu.roll(part[48:72], 127, 1))
-                    total = gelu_of_half(total)
-                    hb_ref[4 * g + o, 0, 2 * j + n] = total[0:16].astype(BF16)
-                    hb_ref[4 * g + o, 1, 2 * j + n] = pltpu.roll(total, 12, 0)[0:16].astype(BF16)
+                [xb_ref[4 * g:4 * g + 4, 4 * j + 2 * n:4 * j + 2 * n + 4].reshape(256, 128) for n in range(2)], axis=1)
+
+            def finish(y, g=g):
+                for o in range(4):
+                    for n in range(2):
+                        cols = slice(n * 128, n * 128 + 128)
+                        total = y[72 * o + 24:72 * o + 48, cols]
+                        total = total + jnp.where(wlane == 0, 0.0, pltpu.roll(y[72 * o:72 * o + 24, cols], 1, 1))
+                        total = total + jnp.where(wlane == 127, 0.0, pltpu.roll(y[72 * o + 48:72 * o + 72, cols], 127, 1))
+                        total = gelu_of_half(total)
+                        if (j, n) == (0, 0):
+                            total = jnp.where(inside[0], total, 0.0)
+                        if (j, n) == (8, 1):
+                            total = jnp.where(inside[1], total, 0.0)
+                        hb_ref[4 * g + o, 0, 2 * j + n] = total[0:16].astype(BF16)
+                        hb_ref[4 * g + o, 1, 2 * j + n] = pltpu.roll(total, 12, 0)[0:16].astype(BF16)
+
+            issue(w1_ref[g], data, finish)
 
     def second_conv(n):
-        k = lax.rem(n + 1, 8)
-        logit = [[None] * 8 for _ in range(2)]
+        k = (n + 1) % 8
         for g in range(4):
             data = jnp.concatenate(
-                [hb_ref[4 * g:4 * g + 4, p, pl.ds(2 * k, 4)].reshape(256, 128) for p in range(2)], axis=1)
-            y = jnp.dot(w2_ref[g], data, preferred_element_type=F32)
-            for z in range(8):
-                for p in range(2):
-                    part = y[24 * z:24 * z + 24, p * 128:p * 128 + 128]
-                    total = part[8:16]
-                    total = total + jnp.where(wlane2 < 2, 0.0, pltpu.roll(part[0:8], 2, 1))
-                    total = total + jnp.where(wlane2 >= 126, 0.0, pltpu.roll(part[16:24], 126, 1))
-                    fe_ref[2 * n + p, g, z] = total
-                    term = dwv[g] * total
-                    logit[p][z] = term if g == 0 else logit[p][z] + term
+                [hb_ref[4 * g:4 * g + 4, p, 2 * k:2 * k + 4].reshape(256, 128) for p in range(2)], axis=1)
+
+            def finish(y, g=g):
+                for z in range(8):
+                    for p in range(2):
+                        cols = slice(p * 128, p * 128 + 128)
+                        total = y[24 * z + 8:24 * z + 16, cols]
+                        total = total + jnp.where(wlane2 < 2, 0.0, pltpu.roll(y[24 * z:24 * z + 8, cols], 2, 1))
+                        total = total + jnp.where(wlane2 >= 126, 0.0, pltpu.roll(y[24 * z + 16:24 * z + 24, cols], 126, 1))
+                        fe_ref[2 * n + p, g, z] = total
+                if g == 3:
+                    optics(n)
+
+            issue(w2_ref[g], data, finish)
+
+    def optics(n):
         for p in range(2):
             subtotal = jnp.zeros((8, 128), F32)
             for z in range(8):
-                x = logit[p][z]
+                x = dwv[0] * fe_ref[2 * n + p, 0, z]
+                for g in range(1, 4):
+                    x = x + dwv[g] * fe_ref[2 * n + p, g, z]
                 x = x + pltpu.roll(x, 4, 0)
                 x = x + pltpu.roll(x, 2, 0)
                 depth = (slab * 8 + z).astype(F32)
@@ -227,9 +259,9 @@
                                             device_id=(peer, tile), device_id_type=MESH)
 
     def to_all(src, dst, sends, recv):
-        @pl.loop(1, ns)
-        def _(d):
-            push(src, dst.at[slab], sends, recv, lax.rem(slab + d, ns)).start()
+        for d in range(1, ns):
+            peer = slab + d
+            push(src, dst.at[slab], sends, recv, peer - jnp.where(peer >= ns, ns, 0)).start()
 
     def from_all(dst, sends, recv):
         every = dst.at[pl.ds(0, ns - 1)]
@@ -246,54 +278,40 @@
         to_all(ts_ref.at[half], tr_ref.at[half], ts_sem.at[half], t_sem.at[half])
 
     relayout(0)
-
-    @pl.loop(0, 2)
-    def _(i):
-        @pl.when(i == 1)
-        def _():
-            relayout(1)
-
-        first_conv(i + 1)
-
-    @pl.loop(2, 9)
-    def _(i):
-        @pl.when(i == 3)
-        def _():
-            relayout(2)
-
-        @pl.when(i == 5)
-        def _():
-            relayout(3)
-
-        @pl.when(i == 6)
-        def _():
-            send_totals(0)
-
-        @pl.when(i == 7)
-        def _():
-            for copy in halos[8:]:
-                copy.wait()
-
-            @pl.loop(0, 16)
-            def _(c):
-                for side in range(2):
-                    for k in range(3):
-                        for blk in range(4):
-                            hs_ref[side, c * 3 + k, 4 * blk:4 * blk + 4, :] = rx_ref[side, blk, c * 3 + k].astype(F32)
-                        xb_ref[c, 35 * side + k] = jnp.where(inside[side], hs_ref[side, c * 3 + k], 0.0).astype(BF16)
-
-        @pl.when((i == 8) & (tile == nt - 1))
-        def _():
-            hb_ref[:, :, 17] = jnp.zeros((16, 2, 16, 128), BF16)
-
-        second_conv(i - 2)
-        first_conv(lax.rem(i + 1, 9))
-
-    @pl.when(tile == 0)
-    def _():
-        hb_ref[:, :, 0] = jnp.zeros((16, 2, 16, 128), BF16)
-
+    first_conv(1)
+    relayout(1)
+    first_conv(2)
+    second_conv(0)
+    first_conv(3)
+    relayout(2)
+    second_conv(1)
+    first_conv(4)
+    second_conv(2)
+    first_conv(5)
+    relayout(3)
+    second_conv(3)
+    first_conv(6)
+    send_totals(0)
+    second_conv(4)
+    first_conv(7)
+
+    for copy in halos[8:]:
+        copy.wait()
+
+    @pl.loop(0, 16)
+    def _(c):
+        for side in range(2):
+            for k in range(3):
+                for blk in range(4):
+                    hs_ref[side, c * 3 + k, 4 * blk:4 * blk + 4, :] = rx_ref[side, blk, c * 3 + k].astype(F32)
+                xb_ref[c, 35 * side + k] = jnp.where(inside[side], hs_ref[side, c * 3 + k], 0.0).astype(BF16)
+
+    second_conv(5)
+    first_conv(8)
+    second_conv(6)
+    first_conv(0)
     second_conv(7)
+    flush()
     send_totals(1)
 
     def shade(half):
@@ -305,7 +323,7 @@
             return total + x, earlier + jnp.where(s < slab, x, 0.0)
 
         zero = jnp.zeros((16, 128), F32)
-        total, earlier = lax.fori_loop(0, ns, gather, (zero, zero))
+        total, earlier = lax.fori_loop(0, ns, gather, (zero, zero), unroll=8)
         ti_ref[...] = 1.0 / total
         ea_ref[...] = earlier
 
@@ -345,19 +363,21 @@
     sb_ref[32] = jnp.zeros((16, 128), BF16)
     shade(0)
 
-    @pl.loop(0, 15)
-    def _(e):
-        send_rows(4 + lax.rem(slab + e, 15))
+    turn = lax.rem(slab, 15)
+    for e in range(15):
+        at = turn + e
+        send_rows(at - jnp.where(at >= 15, 15, 0) + 4)
 
     shade(1)
     below = pltpu.make_async_remote_copy(src_ref=sb_ref.at[0], dst_ref=rb2_ref.at[slab], send_sem=r2s_sem,
                                          recv_sem=r2_sem, device_id=(ns - 1, west), device_id_type=MESH)
     below.start()
 
-    @pl.loop(0, 17)
-    def _(e):
-        at = lax.rem(slab + e, 17)
-        send_rows(at + 15 * ((at + 13) // 17))
+    turn = lax.rem(slab, 17)
+    for e in range(17):
+        at = turn + e
+        at = at - jnp.where(at >= 17, 17, 0)
+        send_rows(at + jnp.where(at >= 4, 15, 0))
 
     rb_ref[slab] = sb_ref[pl.ds(slab, 2)]
     from_all(rb_ref, rs_sem, r_sem)
@@ -406,15 +426,10 @@
     to_all(gs_ref, gb_ref, gs_sem, g_sem)
     from_all(gb_ref, gs_sem, g_sem)
 
-    for half in range(2):
-        @pl.loop(0, ns)
-        def _(s):
-            gf_ref[half, pl.ds(pl.multiple_of(8 * s, 8), 8), :] = gb_ref[s, :, half * 128:half * 128 + 128].astype(F32)
-
-        for color in range(3):
-            for a in range(2):
-                of_ref[color, half, pl.ds(a, 32, stride=2), :] = gf_ref[half, pl.ds(4 * a + color, 32, stride=8), :]
-            out_ref[color, :, half * 128:half * 128 + 128] = of_ref[color, half]
+    rows = jnp.concatenate([gb_ref[k] for k in range(ns)], axis=0)
+    lines = jnp.dot(pm_ref[...], rows, preferred_element_type=F32)
+    for color in range(3):
+        out_ref[color] = lines[64 * color:64 * color + 64]
 
 
 def by_tap(kern):
@@ -449,6 +464,7 @@
                 pltpu.VMEM((4, 288, 256), BF16),
                 pltpu.VMEM((4, 2, 192, 128), F32),
                 pltpu.VMEM((4, 192, 256), BF16),
+                pltpu.VMEM((2, 288, 256), F32),
                 pltpu.VMEM((16, 4, 8, 8, 128), F32),
                 pltpu.VMEM((16, 8, 8, 128), F32),
                 pltpu.VMEM((16, 8, 128), F32),
@@ -468,8 +484,7 @@
                 pltpu.VMEM((8, 256), F32),
                 pltpu.VMEM((8, 256), BF16),
                 pltpu.VMEM((ns, 8, 256), BF16),
-                pltpu.VMEM((2, 8 * ns, 128), F32),
-                pltpu.VMEM((3, 2, 64, 128), F32),
+                pltpu.VMEM((192, 8 * ns), BF16),
                 dma, dma((5,)), dma((14,)), dma((14,)), dma((2,)), dma((2,)), dma, dma, dma, dma, dma, dma,
             ],
             compiler_params=pltpu.CompilerParams(

time: 41.1 us -> 39.8 us (0.968)
  Pallas kernels: 40.3 us -> 38.9 us
    pallas_call x1, Pallas kernels: 40.3 us -> 38.9 us  [body(): pl.pallas_call(lambda *refs: kernel(ns, nt, *refs), out_shape=jax.ShapeDt...]
where the time goes in v4:
time: 39.8 us; the launch traced here: 39.6 us
  Pallas kernels  38.9 us (98%)
  local copies, waits for them, and re-layouts  0.68 us (2%)
    pallas_call x1, Pallas kernels, body(): pl.pallas_call(lambda *refs: kernel(ns, nt, *refs), out_shape=jax.ShapeDt...  38.9 us

profile of v4, /device:TPU:1, one launch (start us, length us, event | category | flops | bytes accessed | tf_op | source)
XLA Modules:
  0.0 39.6 jit_solution(12707250139181087663)
XLA Ops:
  0.0 38.9 %shard_map.64 = f32[3,64,256]{2,1,0:T(8,128)S(1)} custom-call(bf16[27,4,16]{2,1,0:T(4,128)(2,1)} %bitcast.7, bf16[27,4,16]{2,1,0:T(4,128)(2,1)} %bitcast.8, f32[16]{0:T(128)} %refs_2_.1, bf16[3,3,16,16]{3,2,1,0:T(8,128)(2,1)} %refs_3_.1, bf16[3,16]{1,0:T(4,128)(2,1)} %bitcast.9, bf16[16,8,32,128]{3,2,1,0:T(8,128)(2,1)} %refs_5_.1), custom_call_target="tpu_custom_call" | custom-call | tf_op jit(solution)/shard_map/pallas_call | solution.py:445
  39.0 0.7 %copy.8 = f32[3,64,256]{2,1,0:T(8,128)} copy(f32[3,64,256]{2,1,0:T(8,128)S(1)} %shard_map.64) | data formatting | bytes 393216

commit v5 on v4

--- a/solution.py
+++ b/solution.py
@@ -41,6 +41,9 @@
     up, down = lax.rem(slab + 1, ns), lax.rem(slab + ns - 1, ns)
     east, west = lax.rem(tile + 1, nt), lax.rem(tile + nt - 1, nt)
 
+    own = pltpu.make_async_copy(vol_ref, v_ref.at[:, 4:12], vol_sem)
+    own.start()
+
     barrier = pltpu.get_barrier_semaphore()
 
     def greet(s, t):
@@ -50,9 +53,9 @@
         for s in (slab, up, down):
             greet(s, t)
 
-    @pl.loop(1, ns)
-    def _(d):
-        greet(lax.rem(slab + d, ns), tile)
+    for d in range(1, ns):
+        peer = slab + d
+        greet(peer - jnp.where(peer >= ns, ns, 0), tile)
 
     @pl.when(slab == ns - 1)
     def _():
@@ -60,12 +63,24 @@
         def _(s):
             greet(s, east)
 
-    own = pltpu.make_async_copy(vol_ref, v_ref.at[:, 4:12], vol_sem)
-    own.start()
     params = [pltpu.make_async_copy(src, dst, in_sem.at[n]) for n, (src, dst) in enumerate(
         ((k1_any, k1_ref), (k2_any, k2_ref), (dw_any, dw_ref), (up_any, up_ref), (col_any, col_ref)))]
     for copy in params:
         copy.start()
+
+    pl.semaphore_wait(barrier, (ns - 1) + 6 + 1)
+    halos = []
+
+    def send(src, dst, n, s, t):
+        copy = pltpu.make_async_remote_copy(src_ref=src, dst_ref=dst, send_sem=hs_sem.at[n], recv_sem=hr_sem.at[n],
+                                            device_id=(s, t), device_id_type=MESH)
+        copy.start()
+        halos.append(copy)
+
+    for part in range(4):
+        rows = slice(8 * part, 8 * part + 8)
+        send(vol_ref.at[:, 5:8, rows], v_ref.at[:, 1:4, rows], 2 * part, up, tile)
+        send(vol_ref.at[:, 0:3, rows], v_ref.at[:, 12:15, rows], 2 * part + 1, down, tile)
 
     own.wait()
 
@@ -87,20 +102,6 @@
                 for zh in range(2):
                     e_ref[side, zh, c * 3 + k] = f_ref[c, pl.ds((4 + 4 * zh) * 36 + h, 4, stride=36), :].astype(BF16)
 
-    pl.semaphore_wait(barrier, (ns - 1) + 6 + 1)
-    halos = []
-
-    def send(src, dst, n, s, t):
-        copy = pltpu.make_async_remote_copy(src_ref=src, dst_ref=dst, send_sem=hs_sem.at[n], recv_sem=hr_sem.at[n],
-                                            device_id=(s, t), device_id_type=MESH)
-        copy.start()
-        halos.append(copy)
-
-    for part in range(4):
-        rows = slice(8 * part, 8 * part + 8)
-        send(vol_ref.at[:, 5:8, rows], v_ref.at[:, 1:4, rows], 2 * part, up, tile)
-        send(vol_ref.at[:, 0:3, rows], v_ref.at[:, 12:15, rows], 2 * part + 1, down, tile)
-
     send(e_ref.at[1], rx_ref.at[0, 1:3], 8, slab, east)
     send(e_ref.at[0], rx_ref.at[1, 1:3], 9, slab, west)
     send(e_ref.at[1, 1], rx_ref.at[0, 0], 10, up, east)
@@ -386,7 +387,7 @@
     def collect(s, carry):
         return carry + rb_ref[s].astype(F32)
 
-    acc_ref[...] = lax.fori_loop(0, ns, collect, jnp.zeros((2, 16, 128), F32))
+    acc_ref[...] = lax.fori_loop(0, ns, collect, jnp.zeros((2, 16, 128), F32), unroll=8)
 
     @pl.when(slab == ns - 1)
     def _():
@@ -396,7 +397,7 @@
         def collect2(s, carry):
             return carry + rb2_ref[s].astype(F32)
 
-        below_row = lax.fori_loop(0, ns, collect2, jnp.zeros((16, 128), F32))
+        below_row = lax.fori_loop(0, ns, collect2, jnp.zeros((16, 128), F32), unroll=8)
         acc_ref[1] = jnp.where(tile < nt - 1, below_row, 0.0)
 
     lane16 = lax.broadcasted_iota(jnp.int32, (16, 128), 1)

time: 39.8 us -> 39.2 us (0.985)
  Pallas kernels: 38.9 us -> 38.4 us
    pallas_call x1, Pallas kernels: 38.9 us -> 38.4 us  [body(): pl.pallas_call(lambda *refs: kernel(ns, nt, *refs), out_shape=jax.ShapeDt...]
where the time goes in v5:
time: 39.2 us; the launch traced here: 39.1 us
  Pallas kernels  38.4 us (98%)
  local copies, waits for them, and re-layouts  0.68 us (2%)
    pallas_call x1, Pallas kernels, body(): pl.pallas_call(lambda *refs: kernel(ns, nt, *refs), out_shape=jax.ShapeDt...  38.4 us

profile of v5, /device:TPU:1, one launch (start us, length us, event | category | flops | bytes accessed | tf_op | source)
XLA Modules:
  0.0 39.1 jit_solution(4903465364238805182)
XLA Ops:
  0.0 38.4 %shard_map.64 = f32[3,64,256]{2,1,0:T(8,128)S(1)} custom-call(bf16[27,4,16]{2,1,0:T(4,128)(2,1)} %bitcast.7, bf16[27,4,16]{2,1,0:T(4,128)(2,1)} %bitcast.8, f32[16]{0:T(128)} %refs_2_.1, bf16[3,3,16,16]{3,2,1,0:T(8,128)(2,1)} %refs_3_.1, bf16[3,16]{1,0:T(4,128)(2,1)} %bitcast.9, bf16[16,8,32,128]{3,2,1,0:T(8,128)(2,1)} %refs_5_.1), custom_call_target="tpu_custom_call" | custom-call | tf_op jit(solution)/shard_map/pallas_call | solution.py:446
  38.4 0.7 %copy.8 = f32[3,64,256]{2,1,0:T(8,128)} copy(f32[3,64,256]{2,1,0:T(8,128)S(1)} %shard_map.64) | data formatting | bytes 393216

commit v6 on v5

--- a/solution.py
+++ b/solution.py
@@ -69,18 +69,22 @@
         copy.start()
 
     pl.semaphore_wait(barrier, (ns - 1) + 6 + 1)
-    halos = []
+    halos = [None] * 14
 
     def send(src, dst, n, s, t):
         copy = pltpu.make_async_remote_copy(src_ref=src, dst_ref=dst, send_sem=hs_sem.at[n], recv_sem=hr_sem.at[n],
                                             device_id=(s, t), device_id_type=MESH)
         copy.start()
-        halos.append(copy)
-
-    for part in range(4):
+        halos[n] = copy
+
+    def send_layers(part):
         rows = slice(8 * part, 8 * part + 8)
         send(vol_ref.at[:, 5:8, rows], v_ref.at[:, 1:4, rows], 2 * part, up, tile)
         send(vol_ref.at[:, 0:3, rows], v_ref.at[:, 12:15, rows], 2 * part + 1, down, tile)
+
+    send_layers(0)
+    send_layers(1)
+    send_layers(2)
 
     own.wait()
 
@@ -104,6 +108,7 @@
 
     send(e_ref.at[1], rx_ref.at[0, 1:3], 8, slab, east)
     send(e_ref.at[0], rx_ref.at[1, 1:3], 9, slab, west)
+    send_layers(3)
     send(e_ref.at[1, 1], rx_ref.at[0, 0], 10, up, east)
     send(e_ref.at[1, 0], rx_ref.at[0, 3], 11, down, east)
     send(e_ref.at[0, 1], rx_ref.at[1, 0], 12, up, west)

time: 39.2 us -> 39.2 us (level)
  no operation moved by 1% of the time
where the time goes in v6:
time: 39.2 us; the launch traced here: 39.1 us
  Pallas kernels  38.4 us (98%)
  local copies, waits for them, and re-layouts  0.68 us (2%)
    pallas_call x1, Pallas kernels, body(): pl.pallas_call(lambda *refs: kernel(ns, nt, *refs), out_shape=jax.ShapeDt...  38.4 us

profile of v6, /device:TPU:1, one launch (start us, length us, event | category | flops | bytes accessed | tf_op | source)
XLA Modules:
  0.0 39.1 jit_solution(11488862035685784441)
XLA Ops:
  0.0 38.4 %shard_map.64 = f32[3,64,256]{2,1,0:T(8,128)S(1)} custom-call(bf16[27,4,16]{2,1,0:T(4,128)(2,1)} %bitcast.7, bf16[27,4,16]{2,1,0:T(4,128)(2,1)} %bitcast.8, f32[16]{0:T(128)} %refs_2_.1, bf16[3,3,16,16]{3,2,1,0:T(8,128)(2,1)} %refs_3_.1, bf16[3,16]{1,0:T(4,128)(2,1)} %bitcast.9, bf16[16,8,32,128]{3,2,1,0:T(8,128)(2,1)} %refs_5_.1), custom_call_target="tpu_custom_call" | custom-call | tf_op jit(solution)/shard_map/pallas_call | solution.py:451
  38.4 0.7 %copy.8 = f32[3,64,256]{2,1,0:T(8,128)} copy(f32[3,64,256]{2,1,0:T(8,128)S(1)} %shard_map.64) | data formatting | bytes 393216
